TPU v7x, 128 devices: a whole 4x4x4 slice. The times are simulated.
128 devices in a mesh: row: 32 (over z, x, core), col: 4 (over y).
Axes of the slice: x: 4, y: 4, z: 4, core: 2. Of those that a mesh axis runs over, the one named last changes fastest.
Arguments:
- pole_values: float32 [65536], P('row'), may hold values from 0.3 to 127.9, as said below
- rank_one: float32 [65536], P('row'), may hold values from -6 to 6
- deflated: int32 [65536], P('row'), may hold values 0 or 1
- onsite_energy: float32 [65536], P('row'), may hold values from 0.5 to 3
- secular_roots: float32 [16, 256], replicated, may hold values from 0 to 127.7, as said below
- column_order: int32 [16, 256], replicated, may hold values from 0 to 255, each once within a row
- q_blocks: bfloat16 [128, 512, 512], P('row'), may hold values from -1 to 1, as said below
- diag_blocks: float32 [128, 512, 512], P('row'), may hold values from -0.15625 to 0.15625
- coupling_blocks: float32 [128, 512, 512], P('row'), may hold values from -0.15625 to 0.15625
Outputs:
- refined_panel: float32 [16, 65536, 256], P(None, 'row', 'col')
- new_roots: float32 [16, 256], P(None, 'col')
Inputs may be any that keep to these rules, and one draw needn't show every extreme that they name: `pole_values`: every pole lies 0.3 to 0.4 above a multiple of 0.5, at most 0.5 * 256 - 0.1. `secular_roots`: the root of index j in a panel lies between 0.5 j and 0.5 j + 0.2. `q_blocks`: each block is an orthogonal matrix rounded to bfloat16.
All inputs are finite; a program needn't handle non-finite values. No bound on the sum of `deflated` on one device may be relied on, other than what follows from the above.
Results may differ from a plain program's by a relative error of at most 0.0004.
The roundings to bfloat16 on the way count: a program that leaves them out, or rounds other values in their place, can miss the bound.
Values may be sent and summed in bfloat16 or wider, within the bound.
No kernel may reach another device: no remote copies, remote signals or barrier semaphores. Data moves between devices by JAX's collectives and lax.ppermute only.
A program may use at most 192 MiB of HBM per device.

v0:
```python
import functools

import jax
import jax.numpy as jnp
from jax import lax
from jax.experimental import pallas as pl
from jax.experimental.pallas import tpu as pltpu
from jax.sharding import PartitionSpec as P

EPSILON = 1e-06
F32 = jnp.float32
BF16 = jnp.bfloat16
NT = (((1,), (1,)), ((), ()))
NN = (((1,), (0,)), ((), ()))
LANES = 128
MIB = 1 << 20


def dot(a, b, dims):
    return lax.dot_general(a, b, dims, preferred_element_type=F32)


def inverse(d):
    return 1.0 / d


def column_of(row):
    return jnp.transpose(jnp.broadcast_to(row, (LANES, row.shape[1])))


def row_of(column):
    return jnp.sum(jnp.transpose(column), axis=0, keepdims=True)


def joined(ref, p):
    return jnp.concatenate([ref[pl.ds(2 * p, 1), :], ref[pl.ds(2 * p + 1, 1), :]], axis=1)


def split(x):
    high = x.astype(BF16)
    return high, (x - high.astype(F32)).astype(BF16)


def squares_body(place, roots, order, poles, weights, chosen_out, squares_out, lam):
    panels, size = roots.shape
    rows = poles.shape[1]
    own = size // 4
    slots = lax.broadcasted_iota(jnp.int32, (size, size), 1)
    offset = place[0] * own

    def panel(p, carry):
        wanted = column_of(order[pl.ds(p, 1), :].astype(F32)).astype(jnp.int32)
        wanted = jnp.concatenate([wanted, wanted], axis=1)
        values = jnp.broadcast_to(roots[pl.ds(p, 1), :], (size, size))
        picked = jnp.sum(jnp.where(wanted == slots, values, 0.0), axis=1, keepdims=True)
        lam[...] = jnp.broadcast_to(picked, (size, LANES))
        parts = []
        for quarter in range(4):
            start = pl.multiple_of((offset + quarter * own) % size, own)
            here = lam[pl.ds(start, own), :]
            total = jnp.zeros((own, LANES), F32)
            for k in range(rows // LANES):
                lanes = pl.ds(k * LANES, LANES)
                term = weights[:, lanes] * inverse(poles[:, lanes] - here)
                total = total + term * term
            parts.append((here, total))
        for h in range(2):
            here, total = (jnp.concatenate(pair, axis=0) for pair in zip(*parts[2 * h : 2 * h + 2]))
            chosen_out[pl.ds(2 * p + h, 1), :] = jnp.transpose(here)[0:1]
            squares_out[pl.ds(2 * p + h, 1), :] = row_of(total)
        return carry

    lax.fori_loop(0, panels, panel, 0)


def form_body(
    place, chosen, squares, poles, weights, onsite, q, q_before, q_after,
    diag_hbm, coup_hbm, coup_after, formed, sent,
    edge, edge_formed, staged, operated, acc, factors, diag, coup, diagonals, sems,
):
    panels, size = formed.shape[:2]
    block = q.shape[1]
    count = q.shape[0]
    own = size // 4
    chunks = block // LANES
    core = place[1]
    load_diag = pltpu.make_async_copy(diag_hbm, diag, sems.at[0])
    load_coup = pltpu.make_async_copy(coup_hbm, coup, sems.at[1])
    load_diag.start()
    load_coup.start()

    def evaluate(lanes_at, lam, factor):
        lanes = pl.ds(lanes_at, LANES)
        cauchy = weights[:, lanes] * inverse(poles[:, lanes] - lam)
        return (cauchy * factor).astype(BF16)

    def panel(p, carry):
        lam = column_of(joined(chosen, p))
        factor = column_of(lax.rsqrt(joined(squares, p) + EPSILON))
        for b in range(count):
            for k in range(chunks):
                staged[b % 2, :, k * LANES : (k + 1) * LANES] = evaluate(
                    (b + 1) * block + k * LANES, lam, factor
                )
            made = dot(staged[b % 2], q[b], NT)
            formed[p, :, b * block : (b + 1) * block] = made.astype(BF16)
        for side, base in ((0, 0), (1, (count + 1) * block)):
            for k in range(chunks):
                edge[side, pl.ds(p * own, own), k * LANES : (k + 1) * LANES] = evaluate(
                    base + k * LANES, lam[:own], factor[:own]
                )
        return carry

    lax.fori_loop(0, panels, panel, 0)
    edge_formed[0] = dot(edge[0], q_before[...], NT).astype(BF16)
    edge_formed[1] = dot(edge[1], q_after[...], NT).astype(BF16)
    load_diag.wait()
    load_coup.wait()
    diagonals[...] = jnp.zeros(diagonals.shape, F32)

    def own_rows(b):
        if b < 0:
            return edge_formed[0]
        if b == count:
            return edge_formed[1]
        return formed[:, :own, b * block : (b + 1) * block].reshape(panels * own, block)

    for b in range(count):
        d = diag[b]
        terms = [(b, split(0.5 * (d + jnp.transpose(d))), NN), (b - 1, split(coup[b]), NT)]
        if b + 1 < count:
            terms.append((b + 1, split(coup[b + 1]), NN))
        else:
            terms.append((b + 1, (coup_after[...],), NN))
        for n, (source, pieces, dims) in enumerate(terms):
            left = own_rows(source)
            made = dot(left, pieces[0], dims)
            for piece in pieces[1:]:
                made = made + dot(left, piece, dims)
            acc[...] = made if n == 0 else acc[...] + made

        def finish(p, carry, b=b):
            at = pl.ds(p * own, own)
            lam = column_of(joined(chosen, p))[:own]
            g = diagonals[0, at, :]
            h = diagonals[1, at, :]
            for k in range(chunks):
                lanes = pl.ds(b * block + k * LANES, LANES)
                f = formed[p, :own, b * block + k * LANES : b * block + (k + 1) * LANES].astype(F32)
                o = acc[at, k * LANES : (k + 1) * LANES] + onsite[:, lanes] * f
                g = g + f * f
                h = h + f * o
                high, low = split(o - lam * f)
                operated[p, :own, lanes] = high
                operated[p, own:, lanes] = low
            diagonals[0, at, :] = g
            diagonals[1, at, :] = h
            return carry

        lax.fori_loop(0, panels, finish, 0)

    def project(p, carry):
        made = dot(operated[p], formed[p], NT)
        made = made[:own] + made[own:]
        at = pl.ds(p * own, own)
        both = jnp.concatenate([diagonals[0, at, :], diagonals[1, at, :]], axis=0)
        ends = jnp.broadcast_to(row_of(both), (8, LANES))
        rolled = pltpu.roll(ends, own, 1)
        line = lax.broadcasted_iota(jnp.int32, (8, LANES), 0)
        ends = jnp.where(line == 0, ends, rolled)
        half = own // 2
        for h in range(2):
            slot = h ^ core
            sent[slot, p, 0:half, :] = made[h * half : (h + 1) * half, :LANES]
            sent[slot, p, half : 2 * half, :] = made[h * half : (h + 1) * half, LANES:]
            sent[slot, p, 2 * half :, :] = ends
        return carry

    lax.fori_loop(0, panels, project, 0)


def update_body(place, arrived, chosen, sent):
    total = arrived[0]
    for n in range(1, arrived.shape[0]):
        total = total + arrived[n]
    p = place[2]
    half = (total.shape[0] - 8) // 2
    first = place[1] * half
    lam = joined(chosen, p)
    right = column_of(lam)
    right = jnp.where(place[1] == 0, right[:half], right[half : 2 * half])
    line = lax.broadcasted_iota(jnp.int32, (half, LANES), 0) + first
    lane = lax.broadcasted_iota(jnp.int32, (half, LANES), 1)
    same = line == lane
    spacing = right - lam[:, :LANES] + same.astype(F32)
    gram = total[2 * half : 2 * half + 1]
    proj = total[2 * half + 1 : 2 * half + 2]
    low = jnp.where(same, 1.0 + 0.5 * (1.0 - gram), total[:half] / spacing)
    high = total[half : 2 * half] / (right - lam[:, LANES:])
    lane = lax.broadcasted_iota(jnp.int32, (8, LANES), 1)
    inside = (lane >= first) & (lane < first + half)
    ends = jnp.where(inside, proj / jnp.where(inside, gram, 1.0), 0.0)
    made = jnp.concatenate([low, high, ends], axis=0)
    for n in range(sent.shape[0]):
        sent[n] = made


def refine_body(place, mine, other, formed, updated, sums, roots):
    panels, size = formed.shape[:2]
    own = size // 4
    half = own // 2
    zero = place[1] == 0

    def panel(p, carry):
        a, b = mine[p], other[p]
        low = jnp.where(zero, a, b)
        high = jnp.where(zero, b, a)
        u = jnp.concatenate(
            [
                jnp.concatenate([low[:half], low[half:own]], axis=1),
                jnp.concatenate([high[:half], high[half:own]], axis=1),
            ],
            axis=0,
        )
        made = dot(jnp.concatenate(split(u), axis=0), formed[p], NN)
        made = made[:own] + made[own:]
        updated[p] = made
        total = jnp.zeros((own, LANES), F32)
        for k in range(made.shape[1] // LANES):
            piece = made[:, k * LANES : (k + 1) * LANES]
            total = total + piece * piece
        sums[pl.ds(p, 1), :] = row_of(jnp.concatenate([total, jnp.zeros_like(total)], axis=0))
        roots[pl.ds(p, 1), :] = low[own : own + 1] + high[own : own + 1]
        return carry

    lax.fori_loop(0, panels, panel, 0)


def scale_body(sums, updated, refined, scaled, sems, *, order):
    panels, own, rows = updated.shape

    def copy(p):
        return pltpu.make_async_copy(scaled.at[p], refined.at[p], sems.at[p])

    def panel(p, carry):
        factor = column_of(jnp.sqrt(order / sums[pl.ds(p, 1), :]))[:own]
        for k in range(rows // LANES):
            lanes = slice(k * LANES, (k + 1) * LANES)
            scaled[p, :, lanes] = updated[p, :, lanes] * factor
        copy(p).start()
        return carry

    def wait(p, carry):
        copy(p).wait()
        return carry

    lax.fori_loop(0, panels, panel, 0)
    lax.fori_loop(0, panels, wait, 0)


def vmem():
    return pl.BlockSpec(memory_space=pltpu.VMEM)


def smem():
    return pl.BlockSpec(memory_space=pltpu.SMEM)


def hbm():
    return pl.BlockSpec(memory_space=pl.ANY)


def shards(
    pole_values, rank_one, deflated, onsite_energy, secular_roots, column_order,
    q_blocks, diag_blocks, coupling_blocks,
):
    rows = pole_values.shape[0]
    panels, size = secular_roots.shape
    count, block, _ = q_blocks.shape
    own = size // lax.axis_size("col")
    row_count = lax.axis_size("row")
    chips = row_count // 2
    row = lax.axis_index("row")
    place = jnp.stack([lax.axis_index("col"), row % 2, row // 2]).astype(jnp.int32)

    forward = [(i, (i + 1) % row_count) for i in range(row_count)]
    backward = [(i, (i - 1) % row_count) for i in range(row_count)]
    weights = rank_one * (1 - deflated).astype(F32)
    pair = jnp.stack([pole_values, weights])
    q_before = lax.ppermute(q_blocks[count - 1], "row", forward)
    after = lax.ppermute(
        jnp.concatenate([q_blocks[0], coupling_blocks[0].astype(BF16)], axis=0), "row", backward
    )
    pair_before = lax.ppermute(pair[:, rows - block :], "row", forward)
    pair_after = lax.ppermute(pair[:, :block], "row", backward)

    chosen, squares = pl.pallas_call(
        squares_body,
        out_shape=[jax.ShapeDtypeStruct((2 * panels, LANES), F32)] * 2,
        in_specs=[smem()] + [vmem()] * 4,
        out_specs=[vmem()] * 2,
        scratch_shapes=[pltpu.VMEM((size, LANES), F32)],
        compiler_params=pltpu.CompilerParams(vmem_limit_bytes=8 * MIB),
        name="squares",
    )(place, secular_roots, column_order, pole_values[None], weights[None])
    squares = over_rows(squares)

    poles_all = jnp.concatenate([pair_before[0], pole_values, pair_after[0]])[None]
    weights_all = jnp.concatenate(
        [
            jnp.where(row == 0, 0.0, pair_before[1]),
            weights,
            jnp.where(row == row_count - 1, 0.0, pair_after[1]),
        ]
    )[None]
    depth = own + 8
    formed, sent = pl.pallas_call(
        form_body,
        out_shape=[
            pltpu.VMEM((panels, size, rows), BF16),
            jax.ShapeDtypeStruct((2, panels, depth, LANES), F32),
        ],
        in_specs=[smem()] + [vmem()] * 8 + [hbm()] * 2 + [vmem()],
        out_specs=[vmem(), vmem()],
        scratch_shapes=[
            pltpu.VMEM((2, panels * own, block), BF16),
            pltpu.VMEM((2, panels * own, block), BF16),
            pltpu.VMEM((2, size, block), BF16),
            pltpu.VMEM((panels, 2 * own, rows), BF16),
            pltpu.VMEM((panels * own, block), F32),
            pltpu.VMEM((size, LANES), F32),
            pltpu.VMEM((count, block, block), F32),
            pltpu.VMEM((count, block, block), F32),
            pltpu.VMEM((2, panels * own, LANES), F32),
            pltpu.SemaphoreType.DMA((2,)),
        ],
        compiler_params=pltpu.CompilerParams(vmem_limit_bytes=38 * MIB),
        name="form",
    )(
        place, chosen, squares, poles_all, weights_all, onsite_energy[None], q_blocks,
        q_before, after[:block], diag_blocks, coupling_blocks, after[block:],
    )

    swap = [(i, i ^ 1) for i in range(row_count)]
    groups = [[c + 2 * k for k in range(chips)] for c in range(2)]
    spread = functools.partial(
        lax.all_to_all, axis_name="row", split_axis=0, concat_axis=0, tiled=True, axis_index_groups=groups
    )
    arrived = spread(sent[0] + lax.ppermute(sent[1], "row", swap))
    shares = pl.pallas_call(
        update_body,
        out_shape=jax.ShapeDtypeStruct((chips, depth, LANES), F32),
        in_specs=[smem()] + [vmem()] * 2,
        out_specs=vmem(),
        compiler_params=pltpu.CompilerParams(vmem_limit_bytes=8 * MIB),
        name="update",
    )(place, arrived, chosen)
    mine = spread(shares)
    other = lax.ppermute(mine, "row", swap)

    updated, sums, roots = pl.pallas_call(
        refine_body,
        out_shape=[
            pltpu.VMEM((panels, own, rows), F32),
            jax.ShapeDtypeStruct((panels, LANES), F32),
            jax.ShapeDtypeStruct((panels, LANES), F32),
        ],
        in_specs=[smem()] + [vmem()] * 3,
        out_specs=[vmem()] * 3,
        compiler_params=pltpu.CompilerParams(vmem_limit_bytes=12 * MIB),
        name="refine",
    )(place, mine, other, formed)
    refined = pl.pallas_call(
        functools.partial(scale_body, order=float(rows * row_count)),
        out_shape=jax.ShapeDtypeStruct((panels, own, rows), F32),
        in_specs=[vmem()] * 2,
        out_specs=hbm(),
        scratch_shapes=[
            pltpu.VMEM((panels, own, rows), F32),
            pltpu.SemaphoreType.DMA((panels,)),
        ],
        compiler_params=pltpu.CompilerParams(vmem_limit_bytes=12 * MIB),
        name="scale",
    )(over_rows(sums), updated)
    return jnp.transpose(refined, (0, 2, 1)), roots[:, :own]


def over_rows(value):
    def to(step):
        return [(i, step(i // 8, i // 2 % 4, i % 2)) for i in range(32)]

    value = value + lax.ppermute(value, "row", to(lambda z, x, c: z * 8 + x * 2 + 1 - c))
    for move in (
        lambda k: to(lambda z, x, c: z * 8 + (x + k) % 4 * 2 + c),
        lambda k: to(lambda z, x, c: (z + k) % 4 * 8 + x * 2 + c),
    ):
        value = value + sum([lax.ppermute(value, "row", move(k)) for k in (1, 2, 3)])
    return value


def solution(mesh):
    placed = (
        P("row"), P("row"), P("row"), P("row"), P(), P(),
        P("row", None, None), P("row", None, None), P("row", None, None),
    )
    return jax.shard_map(
        shards,
        mesh=mesh,
        in_specs=placed,
        out_specs=(P(None, "row", "col"), P(None, "col")),
        check_vma=False,
    )
```

profile of v0, /device:TPU:0, one launch (start us, length us, event | category | flops | bytes accessed | tf_op | source)
XLA Modules:
  0.0 166.9 jit_solution(7838785003684806753)
XLA Ops:
  0.6 0.7 convert_multiply_fusion
  1.3 0.7 pad_maximum_fusion.4
  2.1 5.9 %collective-permute-start.8 = (f32[2,512]{1,0:T(2,128)S(1)}, f32[2,512]{1,0:T(2,128)S(1)}, u32[]{:S(2)}, u32[]{:S(2)}) collective-permute-start(f32[2,512]{1,0:T(2,128)S(1)} %get-tuple-element.21), channel_id=1, source_target_pairs={{0,124},{4,0},{8,4},{12,8},{16,12},{20,16},{24,20},{28,24},{32,28}... | collective-permute-start | bytes 12296 | tf_op jit(solution)/shard_map/ppermute | solution.py:295
  8.1 0.7 copy-done
  8.8 0.7 copy-done.4
  9.5 0.7 copy-done.5
  10.2 10.2 %squares.1 = (f32[32,128]{1,0:T(8,128)S(1)}, f32[32,128]{1,0:T(8,128)S(1)}) custom-call(s32[3]{0:T(128)S(1)} %pad_add_fusion.place, f32[16,256]{1,0:T(8,128)S(1)} %copy-done.4, s32[16,256]{1,0:T(8,128)S(1)} %copy-done.5, f32[1,2048]{1,0:T(1,128)S(1)} %bitcast.27, f32[1,2048]{1,0:T(1,128)S(1)} %bitcast.25), custom_call_target="tpu_custom_call" | custom-call | tf_op jit(solution)/shard_map/squares/pallas_call | solution.py:297
  20.5 0.6 copy-done.2
  21.1 1.7 %slice_bitcast_fusion.1 = (bf16[512,512]{1,0:T(8,128)(2,1)S(1)}, bf16[512,512]{1,0:T(8,128)(2,1)S(1)}, bf16[512,512]{1,0:T(8,128)(2,1)S(1)}) fusion(bf16[4,512,512]{2,1,0:T(8,128)(2,1)} %q.1, f32[4,512,512]{2,1,0:T(8,128)} %coup_hbm.1), kind=kLoop, calls=%fused_computation.5 | loop fusion | bytes 3145728 | tf_op jit(solution)/shard_map/squeeze | solution.py:292
  22.8 0.6 collective-permute-start.9
  23.4 4.6 %collective-permute-start.10 = (bf16[1024,512]{1,0:T(8,128)(2,1)S(1)}, bf16[1024,512]{1,0:T(8,128)(2,1)S(1)}, u32[]{:S(2)}, u32[]{:S(2)}) collective-permute-start(bf16[1024,512]{1,0:T(8,128)(2,1)S(1)} %pad_maximum_fusion), channel_id=1, source_target_pairs={{0,124},{4,0},{8,4},{12,8},{16,12},{20,16},{24,20},{28,24},{32,28}... | collective-permute-start | bytes 3145736 | tf_op jit(solution)/shard_map/ppermute | solution.py:291
  28.2 0.1 collective-permute-start.2
  28.3 1.9 %collective-permute-start.1 = (f32[32,128]{1,0:T(8,128)S(1)}, f32[32,128]{1,0:T(8,128)S(1)}, u32[]{:S(2)}, u32[]{:S(2)}) collective-permute-start(f32[32,128]{1,0:T(8,128)S(1)} %add.51), channel_id=1, source_target_pairs={{0,8},{4,12},{8,16},{12,20},{16,24},{20,28},{24,0},{28,4},{32,40},... | collective-permute-start | bytes 49160 | tf_op jit(solution)/shard_map/ppermute | solution.py:397
  30.2 0.6 pad_maximum_fusion.1
  30.8 9.9 %collective-permute-done.3 = f32[32,128]{1,0:T(8,128)S(1)} collective-permute-done((f32[32,128]{1,0:T(8,128)S(1)}, f32[32,128]{1,0:T(8,128)S(1)}, u32[]{:S(2)}, u32[]{:S(2)}) %collective-permute-start.3) | collective-permute-done | bytes 16416 | tf_op jit(solution)/shard_map/ppermute | solution.py:397
  40.8 1.0 collective-permute-start.6
  41.8 0.3 collective-permute-start.5
  42.1 1.1 collective-permute-start.4
  43.2 0.6 pad_maximum_fusion.2
  43.8 0.8 collective-permute-done.6
  44.6 2.4 %collective-permute-done.5 = f32[32,128]{1,0:T(8,128)S(1)} collective-permute-done((f32[32,128]{1,0:T(8,128)S(1)}, f32[32,128]{1,0:T(8,128)S(1)}, u32[]{:S(2)}, u32[]{:S(2)}) %collective-permute-start.5) | collective-permute-done | bytes 16416 | tf_op jit(solution)/shard_map/ppermute | solution.py:397
  47.0 0.2 collective-permute-done.4
  47.3 0.6 add_add_fusion.squares
  47.9 1.1 fusion.1
  49.0 0.8 copy-done.8
  49.8 49.1 %form.1 = (bf16[16,256,2048]{2,1,0:T(8,128)(2,1)S(1)}, f32[2,16,72,128]{3,2,1,0:T(8,128)}) custom-call(s32[3]{0:T(128)} %copy-done.6, f32[32,128]{1,0:T(8,128)} %copy-done.2, f32[32,128]{1,0:T(8,128)} %add_add_fusion.squares, f32[1,3072]{1,0:T(1,128)} %bitcast.29, f32[1,3072]{1,0:T(1,128)} %bitcast.30, f32[1,2048]{1,0:T(1,128)} %bitcast.31, ...), custom_call_target="tpu_custom_call" | custom-call | tf_op jit(solution)/shard_map/form/pallas_call | solution.py:317
  98.8 1.1 slice_bitcast_fusion
  100.0 0.3 collective-permute-start.11
  100.3 2.0 %collective-permute-done.11 = f32[16,72,128]{2,1,0:T(8,128)S(1)} collective-permute-done((f32[16,72,128]{2,1,0:T(8,128)S(1)}, f32[16,72,128]{2,1,0:T(8,128)S(1)}, u32[]{:S(2)}, u32[]{:S(2)}) %collective-permute-start.11) | collective-permute-done | bytes 589856 | tf_op jit(solution)/shard_map/ppermute | solution.py:349
  102.3 1.2 bitcast_add_fusion
  103.4 18.9 %all_to_all.10.arrived = f32[16,72,128]{2,1,0:T(8,128)S(1)} all-to-all(f32[16,72,128]{2,1,0:T(8,128)S(1)} %bitcast_add_fusion), channel_id=1, replica_groups={{0,8,16,24,32,40,48,56,64,72,80,88,96,104,112,120},{4,12,20,28,36,44,52..., dimensions={0} | all-to-all | bytes 1179648 | tf_op jit(solution)/shard_map/all_to_all | solution.py:349
  122.3 0.7 update.1
  123.0 14.6 %all_to_all.11.mine = f32[16,72,128]{2,1,0:T(8,128)S(1)} all-to-all(f32[16,72,128]{2,1,0:T(8,128)S(1)} %update.1), channel_id=1, replica_groups={{0,8,16,24,32,40,48,56,64,72,80,88,96,104,112,120},{4,12,20,28,36,44,52..., dimensions={0} | all-to-all | bytes 1179648 | tf_op jit(solution)/shard_map/all_to_all | solution.py:358
  137.7 2.0 %collective-permute-done.12.other = f32[16,72,128]{2,1,0:T(8,128)S(1)} collective-permute-done((f32[16,72,128]{2,1,0:T(8,128)S(1)}, f32[16,72,128]{2,1,0:T(8,128)S(1)}, u32[]{:S(2)}, u32[]{:S(2)}) %collective-permute-start.12) | collective-permute-done | bytes 589856 | tf_op jit(solution)/shard_map/ppermute | solution.py:359
  139.7 7.3 %refine.1 = (f32[16,64,2048]{2,1,0:T(8,128)S(1)}, f32[16,128]{1,0:T(8,128)S(1)}, f32[16,128]{1,0:T(8,128)}) custom-call(s32[3]{0:T(128)S(1)} %copy-done.7, f32[16,72,128]{2,1,0:T(8,128)S(1)} %all_to_all.11.mine, f32[16,72,128]{2,1,0:T(8,128)S(1)} %collective-permute-done.12.other, bf16[16,256,2048]{2,1,0:T(8,128)(2,1)S(1)} %get-tuple-element.12.formed), custom_call_target="tpu_custom_call" | custom-call | tf_op jit(solution)/shard_map/refine/pallas_call | solution.py:361
  147.0 0.1 collective-permute-start.13
  147.1 1.0 collective-permute-done.13
  148.2 1.2 collective-permute-start.16
  149.3 1.5 collective-permute-start.15
  150.9 0.9 collective-permute-done.16
  151.8 2.7 %collective-permute-done.15 = f32[16,128]{1,0:T(8,128)S(1)} collective-permute-done((f32[16,128]{1,0:T(8,128)S(1)}, f32[16,128]{1,0:T(8,128)S(1)}, u32[]{:S(2)}, u32[]{:S(2)}) %collective-permute-start.15) | collective-permute-done | bytes 8224 | tf_op jit(solution)/shard_map/ppermute | solution.py:397
  154.5 1.2 collective-permute-done.14
  155.7 1.1 collective-permute-start.19
  156.8 1.5 collective-permute-start.18
  158.3 1.1 collective-permute-done.19
  159.4 2.6 %collective-permute-done.18 = f32[16,128]{1,0:T(8,128)S(1)} collective-permute-done((f32[16,128]{1,0:T(8,128)S(1)}, f32[16,128]{1,0:T(8,128)S(1)}, u32[]{:S(2)}, u32[]{:S(2)}) %collective-permute-start.18) | collective-permute-done | bytes 8224 | tf_op jit(solution)/shard_map/ppermute | solution.py:397
  162.0 1.2 collective-permute-done.17
  163.2 3.5 %scale.1 = f32[16,64,2048]{2,1,0:T(8,128)} custom-call(f32[16,128]{1,0:T(8,128)S(1)} %add_add_fusion.2.sums, f32[16,64,2048]{2,1,0:T(8,128)S(1)} %get-tuple-element.14.updated), custom_call_target="tpu_custom_call" | custom-call | tf_op jit(solution)/shard_map/scale/pallas_call | solution.py:373
  (35 shorter events, 0.5 us)
Async XLA Ops:
  2.1 26.0 %collective-permute-start.7 = (f32[2,512]{1,0:T(2,128)S(1)}, f32[2,512]{1,0:T(2,128)S(1)}, u32[]{:S(2)}, u32[]{:S(2)}) collective-permute-start(f32[2,512]{1,0:T(2,128)S(1)} %get-tuple-element.20), channel_id=1, source_target_pairs={{0,4},{4,8},{8,12},{12,16},{16,20},{20,24},{24,28},{28,32},{32,36}... | collective-permute-start | bytes 12296 | tf_op jit(solution)/shard_map/ppermute | solution.py:294
  2.1 25.9 %collective-permute-start.8 = (f32[2,512]{1,0:T(2,128)S(1)}, f32[2,512]{1,0:T(2,128)S(1)}, u32[]{:S(2)}, u32[]{:S(2)}) collective-permute-start(f32[2,512]{1,0:T(2,128)S(1)} %get-tuple-element.21), channel_id=1, source_target_pairs={{0,124},{4,0},{8,4},{12,8},{16,12},{20,16},{24,20},{28,24},{32,28}... | collective-permute-start | bytes 12296 | tf_op jit(solution)/shard_map/ppermute | solution.py:295
  8.1 0.7 copy-start
  8.8 0.7 copy-start.4
  9.5 0.7 copy-start.5
  10.2 13.2 %copy-start.6 = (s32[3]{0:T(128)}, s32[3]{0:T(128)S(1)}, u32[]{:S(2)}) copy-start(s32[3]{0:T(128)S(1)} %pad_add_fusion.place) | copy-start | bytes 40
  20.4 0.6 copy-start.2
  21.1 9.2 %copy-start.1 = (f32[2048]{0:T(1024)S(1)}, f32[2048]{0:T(1024)}, u32[]{:S(2)}) copy-start(f32[2048]{0:T(1024)} %param.9) | copy-start | bytes 24580
  21.1 7.0 %collective-permute-start = (f32[32,128]{1,0:T(8,128)S(1)}, f32[32,128]{1,0:T(8,128)S(1)}, u32[]{:S(2)}, u32[]{:S(2)}) collective-permute-start(f32[32,128]{1,0:T(8,128)S(1)} %get-tuple-element.10), channel_id=1, source_target_pairs={{0,4},{4,0},{8,12},{12,8},{16,20},{20,16},{24,28},{28,24},{32,36},... | collective-permute-start | bytes 49160 | tf_op jit(solution)/shard_map/ppermute | solution.py:392
  22.8 26.2 %collective-permute-start.9 = (bf16[512,512]{1,0:T(8,128)(2,1)S(1)}, bf16[512,512]{1,0:T(8,128)(2,1)S(1)}, u32[]{:S(2)}, u32[]{:S(2)}) collective-permute-start(bf16[512,512]{1,0:T(8,128)(2,1)S(1)} %get-tuple-element.17), channel_id=1, source_target_pairs={{0,4},{4,8},{8,12},{12,16},{16,20},{20,24},{24,28},{28,32},{32,36}... | collective-permute-start | bytes 1572872 | tf_op jit(solution)/shard_map/ppermute | solution.py:290
  23.4 24.5 %collective-permute-start.10 = (bf16[1024,512]{1,0:T(8,128)(2,1)S(1)}, bf16[1024,512]{1,0:T(8,128)(2,1)S(1)}, u32[]{:S(2)}, u32[]{:S(2)}) collective-permute-start(bf16[1024,512]{1,0:T(8,128)(2,1)S(1)} %pad_maximum_fusion), channel_id=1, source_target_pairs={{0,124},{4,0},{8,4},{12,8},{16,12},{20,16},{24,20},{28,24},{32,28}... | collective-permute-start | bytes 3145736 | tf_op jit(solution)/shard_map/ppermute | solution.py:291
  28.1 12.6 %collective-permute-start.3 = (f32[32,128]{1,0:T(8,128)S(1)}, f32[32,128]{1,0:T(8,128)S(1)}, u32[]{:S(2)}, u32[]{:S(2)}) collective-permute-start(f32[32,128]{1,0:T(8,128)S(1)} %add.51), channel_id=1, source_target_pairs={{0,24},{4,28},{8,0},{12,4},{16,8},{20,12},{24,16},{28,20},{32,56},... | collective-permute-start | bytes 49160 | tf_op jit(solution)/shard_map/ppermute | solution.py:397
  28.2 12.6 %collective-permute-start.2 = (f32[32,128]{1,0:T(8,128)S(1)}, f32[32,128]{1,0:T(8,128)S(1)}, u32[]{:S(2)}, u32[]{:S(2)}) collective-permute-start(f32[32,128]{1,0:T(8,128)S(1)} %add.51), channel_id=1, source_target_pairs={{0,16},{4,20},{8,24},{12,28},{16,0},{20,4},{24,8},{28,12},{32,48},... | collective-permute-start | bytes 49160 | tf_op jit(solution)/shard_map/ppermute | solution.py:397
  28.3 12.5 %collective-permute-start.1 = (f32[32,128]{1,0:T(8,128)S(1)}, f32[32,128]{1,0:T(8,128)S(1)}, u32[]{:S(2)}, u32[]{:S(2)}) collective-permute-start(f32[32,128]{1,0:T(8,128)S(1)} %add.51), channel_id=1, source_target_pairs={{0,8},{4,12},{8,16},{12,20},{16,24},{20,28},{24,0},{28,4},{32,40},... | collective-permute-start | bytes 49160 | tf_op jit(solution)/shard_map/ppermute | solution.py:397
  40.8 3.8 %collective-permute-start.6 = (f32[32,128]{1,0:T(8,128)S(1)}, f32[32,128]{1,0:T(8,128)S(1)}, u32[]{:S(2)}, u32[]{:S(2)}) collective-permute-start(f32[32,128]{1,0:T(8,128)S(1)} %add_add_fusion.1), channel_id=1, source_target_pairs={{0,96},{4,100},{8,104},{12,108},{16,112},{20,116},{24,120},{28,124... | collective-permute-start | bytes 49160 | tf_op jit(solution)/shard_map/ppermute | solution.py:397
  41.8 5.2 %collective-permute-start.5 = (f32[32,128]{1,0:T(8,128)S(1)}, f32[32,128]{1,0:T(8,128)S(1)}, u32[]{:S(2)}, u32[]{:S(2)}) collective-permute-start(f32[32,128]{1,0:T(8,128)S(1)} %add_add_fusion.1), channel_id=1, source_target_pairs={{0,64},{4,68},{8,72},{12,76},{16,80},{20,84},{24,88},{28,92},{32,9... | collective-permute-start | bytes 49160 | tf_op jit(solution)/shard_map/ppermute | solution.py:397
  42.1 5.2 %collective-permute-start.4 = (f32[32,128]{1,0:T(8,128)S(1)}, f32[32,128]{1,0:T(8,128)S(1)}, u32[]{:S(2)}, u32[]{:S(2)}) collective-permute-start(f32[32,128]{1,0:T(8,128)S(1)} %add_add_fusion.1), channel_id=1, source_target_pairs={{0,32},{4,36},{8,40},{12,44},{16,48},{20,52},{24,56},{28,60},{32,6... | collective-permute-start | bytes 49160 | tf_op jit(solution)/shard_map/ppermute | solution.py:397
  49.0 0.8 copy-start.8
  98.8 23.5 %copy-start.3 = (f32[32,128]{1,0:T(8,128)S(1)}, f32[32,128]{1,0:T(8,128)}, u32[]{:S(2)}) copy-start(f32[32,128]{1,0:T(8,128)} %copy-done.2) | copy-start | bytes 49156
  98.8 23.5 %copy-start.7 = (s32[3]{0:T(128)S(1)}, s32[3]{0:T(128)}, u32[]{:S(2)}) copy-start(s32[3]{0:T(128)} %copy-done.6) | copy-start | bytes 40
  100.0 2.3 %collective-permute-start.11 = (f32[16,72,128]{2,1,0:T(8,128)S(1)}, f32[16,72,128]{2,1,0:T(8,128)S(1)}, u32[]{:S(2)}, u32[]{:S(2)}) collective-permute-start(f32[16,72,128]{2,1,0:T(8,128)S(1)} %slice_bitcast_fusion), channel_id=1, source_target_pairs={{0,4},{4,0},{8,12},{12,8},{16,20},{20,16},{24,28},{28,24},{32,36},... | collective-permute-start | bytes 1769480 | tf_op jit(solution)/shard_map/ppermute | solution.py:349
  137.7 2.0 %collective-permute-start.12 = (f32[16,72,128]{2,1,0:T(8,128)S(1)}, f32[16,72,128]{2,1,0:T(8,128)S(1)}, u32[]{:S(2)}, u32[]{:S(2)}) collective-permute-start(f32[16,72,128]{2,1,0:T(8,128)S(1)} %all_to_all.11.mine), channel_id=1, source_target_pairs={{0,4},{4,0},{8,12},{12,8},{16,20},{20,16},{24,28},{28,24},{32,36},... | collective-permute-start | bytes 1769480 | tf_op jit(solution)/shard_map/ppermute | solution.py:359
  147.0 1.2 collective-permute-start.13
  148.2 3.7 %collective-permute-start.16 = (f32[16,128]{1,0:T(8,128)S(1)}, f32[16,128]{1,0:T(8,128)S(1)}, u32[]{:S(2)}, u32[]{:S(2)}) collective-permute-start(f32[16,128]{1,0:T(8,128)S(1)} %add.59), channel_id=1, source_target_pairs={{0,24},{4,28},{8,0},{12,4},{16,8},{20,12},{24,16},{28,20},{32,56},... | collective-permute-start | bytes 24584 | tf_op jit(solution)/shard_map/ppermute | solution.py:397
  149.3 5.2 %collective-permute-start.15 = (f32[16,128]{1,0:T(8,128)S(1)}, f32[16,128]{1,0:T(8,128)S(1)}, u32[]{:S(2)}, u32[]{:S(2)}) collective-permute-start(f32[16,128]{1,0:T(8,128)S(1)} %add.59), channel_id=1, source_target_pairs={{0,16},{4,20},{8,24},{12,28},{16,0},{20,4},{24,8},{28,12},{32,48},... | collective-permute-start | bytes 24584 | tf_op jit(solution)/shard_map/ppermute | solution.py:397
  150.8 4.9 %collective-permute-start.14 = (f32[16,128]{1,0:T(8,128)S(1)}, f32[16,128]{1,0:T(8,128)S(1)}, u32[]{:S(2)}, u32[]{:S(2)}) collective-permute-start(f32[16,128]{1,0:T(8,128)S(1)} %add.59), channel_id=1, source_target_pairs={{0,8},{4,12},{8,16},{12,20},{16,24},{20,28},{24,0},{28,4},{32,40},... | collective-permute-start | bytes 24584 | tf_op jit(solution)/shard_map/ppermute | solution.py:397
  155.7 3.7 %collective-permute-start.19 = (f32[16,128]{1,0:T(8,128)S(1)}, f32[16,128]{1,0:T(8,128)S(1)}, u32[]{:S(2)}, u32[]{:S(2)}) collective-permute-start(f32[16,128]{1,0:T(8,128)S(1)} %add_add_fusion.3), channel_id=1, source_target_pairs={{0,96},{4,100},{8,104},{12,108},{16,112},{20,116},{24,120},{28,124... | collective-permute-start | bytes 24584 | tf_op jit(solution)/shard_map/ppermute | solution.py:397
  156.8 5.2 %collective-permute-start.18 = (f32[16,128]{1,0:T(8,128)S(1)}, f32[16,128]{1,0:T(8,128)S(1)}, u32[]{:S(2)}, u32[]{:S(2)}) collective-permute-start(f32[16,128]{1,0:T(8,128)S(1)} %add_add_fusion.3), channel_id=1, source_target_pairs={{0,64},{4,68},{8,72},{12,76},{16,80},{20,84},{24,88},{28,92},{32,9... | collective-permute-start | bytes 24584 | tf_op jit(solution)/shard_map/ppermute | solution.py:397
  158.3 4.9 %collective-permute-start.17 = (f32[16,128]{1,0:T(8,128)S(1)}, f32[16,128]{1,0:T(8,128)S(1)}, u32[]{:S(2)}, u32[]{:S(2)}) collective-permute-start(f32[16,128]{1,0:T(8,128)S(1)} %add_add_fusion.3), channel_id=1, source_target_pairs={{0,32},{4,36},{8,40},{12,44},{16,48},{20,52},{24,56},{28,60},{32,6... | collective-permute-start | bytes 24584 | tf_op jit(solution)/shard_map/ppermute | solution.py:397
where the time goes:
time: 168 us; the launch traced here: 167 us
  Pallas kernels  70.8 us (42%)
  blocking collectives  33.5 us (20%)
  waiting for transfers between devices  28.1 us (17%)
  starting transfers between devices  21.4 us (13%)
  local copies, waits for them, and re-layouts  7.43 us (4%)
  other arithmetic  4.59 us (3%)
    pallas_call x1, Pallas kernels, shards(): pl.pallas_call(form_body, out_shape=[pltpu.VMEM((panels, size, rows), BF1...  49.1 us
    ppermute x12, waiting for transfers between devices, over_rows(): lax.ppermute(value, 'row', move(k))  23 us
    all_to_all x1, blocking collectives, shards(): arrived = spread(sent[0] + lax.ppermute(sent[1], 'row', swap))  18.9 us
    all_to_all x1, blocking collectives, shards(): mine = spread(shares)  14.6 us
    pallas_call x1, Pallas kernels, shards(): pl.pallas_call(squares_body, out_shape=[jax.ShapeDtypeStruct((2 * panels,...  10.2 us
    ppermute x12, starting transfers between devices, over_rows(): lax.ppermute(value, 'row', move(k))  9.87 us
    pallas_call x1, Pallas kernels, shards(): pl.pallas_call(refine_body, out_shape=[pltpu.VMEM((panels, own, rows), F3...  7.33 us
    ppermute x1, starting transfers between devices, shards(): pair_after = lax.ppermute(pair[:, :block], 'row', backward)  5.85 us
  transfers between devices with their start and end apart: 20, of which 13 were waited for; matrix products, arithmetic and copies ran while one was open for 3% of the time, Pallas kernels for 6%

commit v1 on v0

v1 whole, which is shorter than its diff:
```python
import functools

import jax
import jax.numpy as jnp
from jax import lax
from jax.experimental import pallas as pl
from jax.experimental.pallas import tpu as pltpu
from jax.sharding import PartitionSpec as P


EPSILON = 1e-06
F32 = jnp.float32
BF16 = jnp.bfloat16
NT = (((1,), (1,)), ((), ()))
NN = (((1,), (0,)), ((), ()))
LANES = 128
MIB = 1 << 20


def dot(a, b, dims):
    return lax.dot_general(a, b, dims, preferred_element_type=F32)


def inverse(d):
    return 1.0 / d


def column_of(row):
    return jnp.transpose(jnp.broadcast_to(row, (LANES, row.shape[1])))


def row_of(column):
    return jnp.sum(jnp.transpose(column), axis=0, keepdims=True)


def joined(ref, p):
    return jnp.concatenate([ref[pl.ds(2 * p, 1), :], ref[pl.ds(2 * p + 1, 1), :]], axis=1)


def split(x):
    high = x.astype(BF16)
    return high, (x - high.astype(F32)).astype(BF16)


def fetch(pairs, sems):
    copies = [pltpu.make_async_copy(src, dst, sems.at[n]) for n, (src, dst) in enumerate(pairs)]
    for copy in copies:
        copy.start()
    return copies


def squares_body(
    place, roots_hbm, order_hbm, poles_hbm, rank_hbm, deflated_hbm, chosen_out, columns_out, squares_out,
    roots, order, poles, rank, deflated, weights, picked, sems,
):
    panels, size = roots.shape
    rows = poles.shape[1]
    own = size // 4
    for copy in fetch(
        [(roots_hbm, roots), (order_hbm, order), (poles_hbm, poles), (rank_hbm, rank), (deflated_hbm, deflated)],
        sems,
    ):
        copy.wait()
    weights[...] = rank[...] * (1 - deflated[...]).astype(F32)
    slots = lax.broadcasted_iota(jnp.int32, (size, size), 1)
    offset = place[0] * own

    def pick(p, slot):
        wanted = column_of(order[pl.ds(p, 1), :].astype(F32)).astype(jnp.int32)
        wanted = jnp.concatenate([wanted, wanted], axis=1)
        values = jnp.broadcast_to(roots[pl.ds(p, 1), :], (size, size))
        value = jnp.sum(jnp.where(wanted == slots, values, 0.0), axis=1, keepdims=True)
        picked[slot] = jnp.broadcast_to(value, (size, LANES))

    def add_up(p, slot):
        parts = []
        for quarter in range(4):
            start = pl.multiple_of((offset + quarter * own) % size, own)
            here = picked[slot, pl.ds(start, own), :]
            columns_out[p, quarter * own : (quarter + 1) * own, :] = here
            total = jnp.zeros((own, LANES), F32)
            for k in range(rows // LANES):
                lanes = pl.ds(k * LANES, LANES)
                term = weights[:, lanes] * inverse(poles[:, lanes] - here)
                total = total + term * term
            parts.append((here, total))
        for h in range(2):
            here, total = (jnp.concatenate(pair, axis=0) for pair in zip(*parts[2 * h : 2 * h + 2]))
            chosen_out[pl.ds(2 * p + h, 1), :] = jnp.transpose(here)[0:1]
            squares_out[pl.ds(2 * p + h, 1), :] = row_of(total)

    def two(i, carry):
        pick(2 * i + 1, 1)
        add_up(2 * i, 0)
        pick(jnp.minimum(2 * i + 2, panels - 1), 0)
        add_up(2 * i + 1, 1)
        return carry

    pick(0, 0)
    lax.fori_loop(0, panels // 2, two, 0)


def form_body(
    place, columns, squares_a, squares_b, squares_c, squares_d, poles_hbm, rank_hbm, deflated_hbm, onsite_hbm,
    pair_before, pair_after, q_hbm, before_hbm, after_hbm, diag_hbm, coup_hbm,
    formed, kept, sent,
    staged, edge_formed, operated, acc, factors, squares, diag, coup, q, before, after, sym_parts, coup_parts,
    poles, rank, deflated, weights, onsite, grams, sems,
):
    panels, size = formed.shape[:2]
    count, block = q.shape[:2]
    own = size // 4
    chunks = block // LANES
    core = place[1]
    copies = fetch(
        [
            (poles_hbm, poles), (rank_hbm, rank), (deflated_hbm, deflated), (onsite_hbm, onsite),
            (q_hbm, q), (before_hbm, before), (after_hbm, after), (diag_hbm, diag), (coup_hbm, coup),
        ],
        sems,
    )
    squares[...] = squares_a[...] + squares_b[...] + squares_c[...] + squares_d[...]
    for copy in copies[:4]:
        copy.wait()
    weights[...] = rank[...] * (1 - deflated[...]).astype(F32)

    def prepare(p, slot):
        factors[slot] = column_of(lax.rsqrt(joined(squares, p) + EPSILON))

    def evaluate(p, slot):
        lam = columns[p]
        factor = factors[slot]
        for k in range(count * chunks):
            lanes = slice(k * LANES, (k + 1) * LANES)
            cauchy = weights[:, lanes] * inverse(poles[:, lanes] - lam)
            staged[slot, :, lanes] = (cauchy * factor).astype(BF16)
        for side, pair in enumerate((pair_before, pair_after)):
            for k in range(chunks):
                lanes = slice(k * LANES, (k + 1) * LANES)
                cauchy = pair[1:2, lanes] * inverse(pair[0:1, lanes] - lam[:own])
                operated[p, side * own : (side + 1) * own, lanes] = (cauchy * factor[:own]).astype(BF16)

    def multiply(p, slot):
        for b in range(count):
            lanes = slice(b * block, (b + 1) * block)
            formed[p, :, lanes] = dot(staged[slot, :, lanes], q[b], NT).astype(BF16)

    last = panels - 1

    def two(i, carry):
        p = 2 * i
        multiply(p, 0)
        evaluate(p + 1, 1)
        prepare(jnp.minimum(p + 2, last), 0)
        multiply(p + 1, 1)
        evaluate(jnp.minimum(p + 2, last), 0)
        prepare(jnp.minimum(p + 3, last), 1)
        return carry

    prepare(0, 0)
    prepare(1, 1)
    evaluate(0, 0)
    copies[4].wait()
    lax.fori_loop(0, panels // 2, two, 0)
    for copy in copies[5:]:
        copy.wait()
    for side, blocks in ((0, before[...]), (1, after[:block])):
        left = operated[:, side * own : (side + 1) * own, :block].reshape(panels * own, block)
        edge_formed[side] = dot(left, blocks, NT).astype(BF16)

    def own_rows(b):
        if b < 0:
            return edge_formed[0]
        if b == count:
            return edge_formed[1]
        return formed[:, :own, b * block : (b + 1) * block].reshape(panels * own, block)

    eye = lax.broadcasted_iota(jnp.int32, (LANES, LANES), 0) == lax.broadcasted_iota(jnp.int32, (LANES, LANES), 1)

    def ready_sym(b):
        for m in range(chunks):
            for n in range(m, chunks):
                at = slice(m * LANES, (m + 1) * LANES)
                to = slice(n * LANES, (n + 1) * LANES)
                value = 0.5 * (diag[b, at, to] + jnp.transpose(diag[b, to, at]))
                if m == n:
                    level = onsite[:, b * block + m * LANES : b * block + (m + 1) * LANES]
                    value = value + jnp.where(eye, level, 0.0)
                high, low = split(value)
                sym_parts[b % 2, 0, at, to] = high
                sym_parts[b % 2, 1, at, to] = low
                if m != n:
                    high, low = split(jnp.transpose(value))
                    sym_parts[b % 2, 0, to, at] = high
                    sym_parts[b % 2, 1, to, at] = low

    def ready_coup(b):
        high, low = split(coup[b])
        coup_parts[b, 0] = high
        coup_parts[b, 1] = low

    def apply(b):
        terms = [
            (own_rows(b), (sym_parts[b % 2, 0], sym_parts[b % 2, 1]), NN),
            (own_rows(b - 1), (coup_parts[b, 0], coup_parts[b, 1]), NT),
        ]
        if b + 1 < count:
            terms.append((own_rows(b + 1), (coup_parts[b + 1, 0], coup_parts[b + 1, 1]), NN))
        else:
            terms.append((own_rows(b + 1), (after[block:],), NN))
        made = None
        for left, pieces, dims in terms:
            for piece in pieces:
                term = dot(left, piece, dims)
                made = term if made is None else made + term
        acc[b % 2] = made

    def finish(b):
        for p in range(panels):
            at = slice(p * own, (p + 1) * own)
            lam = columns[p, :own]
            g = None if b == 0 else grams[at]
            for k in range(chunks):
                lanes = slice(b * block + k * LANES, b * block + (k + 1) * LANES)
                f = formed[p, :own, lanes].astype(F32)
                high, low = split(acc[b % 2, at, k * LANES : (k + 1) * LANES] - lam * f)
                g = f * f if g is None else g + f * f
                operated[p, :own, lanes] = high
                operated[p, own:, lanes] = low
            grams[at] = g

    ready_sym(0)
    ready_coup(0)
    ready_coup(1)
    for b in range(count):
        apply(b)
        if b + 1 < count:
            ready_sym(b + 1)
        if b + 2 < count:
            ready_coup(b + 2)
        if b > 0:
            finish(b - 1)
    finish(count - 1)

    half = own // 2

    def project(p):
        made = dot(operated[p], formed[p], NT)
        made = made[:own] + made[own:]
        g = grams[pl.ds(pl.multiple_of(p * own, own), own), :]
        ends = jnp.broadcast_to(row_of(jnp.concatenate([g, jnp.zeros_like(g)], axis=0)), (8, LANES))
        parts = [
            jnp.concatenate([made[h * half : (h + 1) * half, :LANES], made[h * half : (h + 1) * half, LANES:], ends], axis=0)
            for h in range(2)
        ]
        first = core == 0
        kept[p] = jnp.where(first, parts[0], parts[1])
        sent[p] = jnp.where(first, parts[1], parts[0])

    def project_two(i, carry):
        project(2 * i)
        project(2 * i + 1)
        return carry

    lax.fori_loop(0, panels // 2, project_two, 0)


def update_body(place, arrived, chosen, sent):
    total = arrived[0]
    for n in range(1, arrived.shape[0]):
        total = total + arrived[n]
    p = place[2]
    half = (total.shape[0] - 8) // 2
    first = place[1] * half
    lam = joined(chosen, p)
    right = column_of(lam)
    right = jnp.where(place[1] == 0, right[:half], right[half : 2 * half])
    line = lax.broadcasted_iota(jnp.int32, (half, LANES), 0) + first
    lane = lax.broadcasted_iota(jnp.int32, (half, LANES), 1)
    same = line == lane
    spacing = right - lam[:, :LANES] + same.astype(F32)
    gram = total[2 * half : 2 * half + 1]
    numerator = total[:half]
    low = jnp.where(same, 1.0 + 0.5 * (1.0 - gram), numerator / spacing)
    high = total[half : 2 * half] / (right - lam[:, LANES:])
    roots = jnp.where(same, numerator / jnp.where(same, gram, 1.0) + right, 0.0)
    ends = jnp.broadcast_to(jnp.sum(roots, axis=0, keepdims=True), (8, LANES))
    made = jnp.concatenate([low, high, ends], axis=0)
    for n in range(sent.shape[0]):
        sent[n] = made


def refine_body(place, mine, other, formed, updated, sums, roots):
    panels, size = formed.shape[:2]
    own = size // 4
    half = own // 2
    zero = place[1] == 0

    def panel(p):
        a, b = mine[p], other[p]
        low = jnp.where(zero, a, b)
        high = jnp.where(zero, b, a)
        u = jnp.concatenate(
            [
                jnp.concatenate([low[:half], low[half:own]], axis=1),
                jnp.concatenate([high[:half], high[half:own]], axis=1),
            ],
            axis=0,
        )
        made = dot(jnp.concatenate(split(u), axis=0), formed[p], NN)
        made = made[:own] + made[own:]
        updated[p] = made
        total = jnp.zeros((own, LANES), F32)
        for k in range(made.shape[1] // LANES):
            piece = made[:, k * LANES : (k + 1) * LANES]
            total = total + piece * piece
        sums[pl.ds(p, 1), :] = row_of(jnp.concatenate([total, jnp.zeros_like(total)], axis=0))
        roots[pl.ds(p, 1), :] = low[own : own + 1] + high[own : own + 1]

    def two(i, carry):
        panel(2 * i)
        panel(2 * i + 1)
        return carry

    lax.fori_loop(0, panels // 2, two, 0)


def scale_body(sums_a, sums_b, sums_c, sums_d, updated, refined, sums, scaled, sems, *, order):
    panels, own, rows = updated.shape
    sums[...] = sums_a[...] + sums_b[...] + sums_c[...] + sums_d[...]

    def copy(p):
        return pltpu.make_async_copy(scaled.at[p], refined.at[p], sems.at[p])

    def panel(p, carry):
        factor = column_of(jnp.sqrt(order / sums[pl.ds(p, 1), :]))[:own]
        for k in range(rows // LANES):
            lanes = slice(k * LANES, (k + 1) * LANES)
            scaled[p, :, lanes] = updated[p, :, lanes] * factor
        copy(p).start()
        return carry

    def wait(p, carry):
        copy(p).wait()
        return carry

    lax.fori_loop(0, panels, panel, 0)
    lax.fori_loop(0, panels, wait, 0)


def vmem():
    return pl.BlockSpec(memory_space=pltpu.VMEM)


def smem():
    return pl.BlockSpec(memory_space=pltpu.SMEM)


def hbm():
    return pl.BlockSpec(memory_space=pltpu.HBM)


def shards(
    pole_values, rank_one, deflated, onsite_energy, secular_roots, column_order,
    q_blocks, diag_blocks, coupling_blocks,
):
    rows = pole_values.shape[0]
    panels, size = secular_roots.shape
    count, block, _ = q_blocks.shape
    own = size // lax.axis_size("col")
    row_count = lax.axis_size("row")
    chips = row_count // 2
    row = lax.axis_index("row")
    place = jnp.stack([lax.axis_index("col"), row % 2, row // 2]).astype(jnp.int32)

    forward = [(i, (i + 1) % row_count) for i in range(row_count)]
    backward = [(i, (i - 1) % row_count) for i in range(row_count)]
    weights = rank_one * (1 - deflated).astype(F32)
    pair = jnp.stack([pole_values, weights])
    before = lax.ppermute(q_blocks[count - 1], "row", forward)
    after = lax.ppermute(
        jnp.concatenate([q_blocks[0], coupling_blocks[0].astype(BF16)], axis=0), "row", backward
    )
    ends = jnp.stack([row == 0, row == row_count - 1])
    pair_before = lax.ppermute(pair[:, rows - block :], "row", forward)
    pair_after = lax.ppermute(pair[:, :block], "row", backward)
    pair_before, pair_after = (
        jnp.stack([near[0], jnp.where(end, 0.0, near[1])])
        for near, end in ((pair_before, ends[0]), (pair_after, ends[1]))
    )
    vectors = (pole_values[None], rank_one[None], deflated[None])

    chosen, columns, squares = pl.pallas_call(
        squares_body,
        out_shape=[
            pltpu.VMEM((2 * panels, LANES), F32),
            pltpu.VMEM((panels, size, LANES), F32),
            pltpu.VMEM((2 * panels, LANES), F32),
        ],
        in_specs=[smem()] + [hbm()] * 5,
        out_specs=[vmem()] * 3,
        scratch_shapes=[
            pltpu.VMEM((panels, size), F32),
            pltpu.VMEM((panels, size), jnp.int32),
            pltpu.VMEM((1, rows), F32),
            pltpu.VMEM((1, rows), F32),
            pltpu.VMEM((1, rows), jnp.int32),
            pltpu.VMEM((1, rows), F32),
            pltpu.VMEM((2, size, LANES), F32),
            pltpu.SemaphoreType.DMA((5,)),
        ],
        compiler_params=pltpu.CompilerParams(vmem_limit_bytes=8 * MIB),
        name="squares",
    )(place, secular_roots, column_order, *vectors)

    depth = own + 8
    formed, kept, sent = pl.pallas_call(
        form_body,
        out_shape=[
            pltpu.VMEM((panels, size, rows), BF16),
            pltpu.VMEM((panels, depth, LANES), F32),
            pltpu.VMEM((panels, depth, LANES), F32),
        ],
        in_specs=[smem()] + [vmem()] * 5 + [hbm()] * 4 + [vmem()] * 2 + [hbm()] * 5,
        out_specs=[vmem()] * 3,
        scratch_shapes=[
            pltpu.VMEM((2, size, rows), BF16),
            pltpu.VMEM((2, panels * own, block), BF16),
            pltpu.VMEM((panels, 2 * own, rows), BF16),
            pltpu.VMEM((2, panels * own, block), F32),
            pltpu.VMEM((2, size, LANES), F32),
            pltpu.VMEM((2 * panels, LANES), F32),
            pltpu.VMEM((count, block, block), F32),
            pltpu.VMEM((count, block, block), F32),
            pltpu.VMEM((count, block, block), BF16),
            pltpu.VMEM((block, block), BF16),
            pltpu.VMEM((2 * block, block), BF16),
            pltpu.VMEM((2, 2, block, block), BF16),
            pltpu.VMEM((count, 2, block, block), BF16),
            pltpu.VMEM((1, rows), F32),
            pltpu.VMEM((1, rows), F32),
            pltpu.VMEM((1, rows), jnp.int32),
            pltpu.VMEM((1, rows), F32),
            pltpu.VMEM((1, rows), F32),
            pltpu.VMEM((panels * own, LANES), F32),
            pltpu.SemaphoreType.DMA((9,)),
        ],
        compiler_params=pltpu.CompilerParams(vmem_limit_bytes=42 * MIB),
        name="form",
    )(
        place, columns, *over_rows(squares), *vectors, onsite_energy[None], pair_before, pair_after,
        q_blocks, before, after, diag_blocks, coupling_blocks,
    )

    swap = [(i, i ^ 1) for i in range(row_count)]
    groups = [[c + 2 * k for k in range(chips)] for c in range(2)]
    spread = functools.partial(
        lax.all_to_all, axis_name="row", split_axis=0, concat_axis=0, tiled=True, axis_index_groups=groups
    )
    arrived = spread(kept + lax.ppermute(sent, "row", swap))
    shares = pl.pallas_call(
        update_body,
        out_shape=jax.ShapeDtypeStruct((chips, depth, LANES), F32),
        in_specs=[smem()] + [vmem()] * 2,
        out_specs=vmem(),
        compiler_params=pltpu.CompilerParams(vmem_limit_bytes=8 * MIB),
        name="update",
    )(place, arrived, chosen)
    mine = spread(shares)
    other = lax.ppermute(mine, "row", swap)

    updated, sums, roots = pl.pallas_call(
        refine_body,
        out_shape=[
            pltpu.VMEM((panels, own, rows), F32),
            pltpu.VMEM((panels, LANES), F32),
            jax.ShapeDtypeStruct((panels, LANES), F32),
        ],
        in_specs=[smem()] + [vmem()] * 3,
        out_specs=[vmem()] * 3,
        compiler_params=pltpu.CompilerParams(vmem_limit_bytes=12 * MIB),
        name="refine",
    )(place, mine, other, formed)
    refined = pl.pallas_call(
        functools.partial(scale_body, order=float(rows * row_count)),
        out_shape=jax.ShapeDtypeStruct((panels, own, rows), F32),
        in_specs=[vmem()] * 5,
        out_specs=hbm(),
        scratch_shapes=[
            pltpu.VMEM((panels, LANES), F32),
            pltpu.VMEM((panels, own, rows), F32),
            pltpu.SemaphoreType.DMA((panels,)),
        ],
        compiler_params=pltpu.CompilerParams(vmem_limit_bytes=12 * MIB),
        name="scale",
    )(*over_rows(sums), updated)
    return jnp.transpose(refined, (0, 2, 1)), roots[:, :own]


def over_rows(value):
    def to(step):
        return [(i, step(i // 8, i // 2 % 4, i % 2)) for i in range(32)]

    value = value + lax.ppermute(value, "row", to(lambda z, x, c: z * 8 + x * 2 + 1 - c))
    along_x = [to(lambda z, x, c, k=k: z * 8 + (x + k) % 4 * 2 + c) for k in (1, 2, 3)]
    value = value + sum([lax.ppermute(value, "row", move) for move in along_x])
    along_z = [to(lambda z, x, c, k=k: (z + k) % 4 * 8 + x * 2 + c) for k in (1, 2, 3)]
    return [value] + [lax.ppermute(value, "row", move) for move in along_z]


def solution(mesh):
    placed = (
        P("row"), P("row"), P("row"), P("row"), P(), P(),
        P("row", None, None), P("row", None, None), P("row", None, None),
    )
    return jax.shard_map(
        shards,
        mesh=mesh,
        in_specs=placed,
        out_specs=(P(None, "row", "col"), P(None, "col")),
        check_vma=False,
    )
```

time: 168 us -> 140 us (0.83)
  Pallas kernels: 70.8 us -> 57.7 us
  waiting for transfers between devices: 28.1 us -> 23.9 us
  other arithmetic: 4.59 us -> 0.88 us
  local copies, waits for them, and re-layouts: 7.43 us -> 4.75 us
    pallas_call x1, Pallas kernels: 49.1 us -> 38.4 us  [shards(): pl.pallas_call(form_body, out_shape=[pltpu.VMEM((panels, size, rows), BF1...]
    ppermute x14, waiting for transfers between devices: 25 us -> 19.7 us  [the longest x6 9.15 us: over_rows(): value = value + sum([lax.ppermute(value, 'row', move) for move in along_x])]
    ppermute x1, starting transfers between devices: 5.85 us -> 0.74 us  [shards(): pair_after = lax.ppermute(pair[:, :block], 'row', backward)]
    ppermute x14, starting transfers between devices: 10.7 us -> 13.4 us  [the longest x6 8.47 us: over_rows(): return [value] + [lax.ppermute(value, 'row', move) for move in along_z]]
    pallas_call x1, Pallas kernels: 7.33 us -> 5.44 us  [shards(): pl.pallas_call(refine_body, out_shape=[pltpu.VMEM((panels, own, rows), F3...]
    add x5 -> x3, other arithmetic: 1.79 us -> 0.1 us  [the longest x1 0.08 us: shards(): arrived = spread(kept + lax.ppermute(sent, 'row', swap))]
    unnamed x18 -> x30, local copies, waits for them, and re-layouts: 3.54 us -> 3.05 us
  transfers between devices with their start and end apart: 20 -> 20, of which waited for: 13 -> 15; matrix products, arithmetic and copies ran while one was open for 3% -> 1% of each run, Pallas kernels for 6% -> 7%
where the time goes in v1:
time: 140 us
  Pallas kernels  57.7 us (41%)
  blocking collectives  31.9 us (23%)
  waiting for transfers between devices  23.9 us (17%)
  starting transfers between devices  20.1 us (14%)
  local copies, waits for them, and re-layouts  4.75 us (3%)
    pallas_call x1, Pallas kernels, shards(): pl.pallas_call(form_body, out_shape=[pltpu.VMEM((panels, size, rows), BF1...  38.4 us
    all_to_all x1, blocking collectives, shards(): arrived = spread(kept + lax.ppermute(sent, 'row', swap))  17.2 us
    all_to_all x1, blocking collectives, shards(): mine = spread(shares)  14.6 us
    pallas_call x1, Pallas kernels, shards(): pl.pallas_call(squares_body, out_shape=[pltpu.VMEM((2 * panels, LANES), F...  9.67 us
    ppermute x6, waiting for transfers between devices, over_rows(): value = value + sum([lax.ppermute(value, 'row', move) for move in along_x])  9.15 us
    ppermute x6, waiting for transfers between devices, over_rows(): return [value] + [lax.ppermute(value, 'row', move) for move in along_z]  8.55 us
    ppermute x6, starting transfers between devices, over_rows(): return [value] + [lax.ppermute(value, 'row', move) for move in along_z]  8.47 us
    ppermute x1, starting transfers between devices, shards(): lax.ppermute(jnp.concatenate([q_blocks[0], coupling_blocks[0].astype(BF16...  5.85 us
  transfers between devices with their start and end apart: 20, of which 15 were waited for; matrix products, arithmetic and copies ran while one was open for 1% of the time, Pallas kernels for 7%

profile of v1, /device:TPU:0, one launch (start us, length us, event | category | flops | bytes accessed | tf_op | source)
XLA Modules:
  0.0 140.2 jit_solution(16779552708299958730)
XLA Ops:
  0.6 0.0 copy-start.3
  0.7 1.7 %slice_bitcast_fusion = (bf16[512,512]{1,0:T(8,128)(2,1)S(1)}, bf16[512,512]{1,0:T(8,128)(2,1)S(1)}, bf16[512,512]{1,0:T(8,128)(2,1)S(1)}) fusion(bf16[4,512,512]{2,1,0:T(8,128)(2,1)} %q_hbm.1, f32[4,512,512]{2,1,0:T(8,128)} %coup_hbm.1), kind=kLoop, calls=%fused_computation.3 | loop fusion | bytes 3145728 | tf_op jit(solution)/shard_map/squeeze | solution.py:382
  2.4 0.1 pad_maximum_fusion
  2.5 5.9 %collective-permute-start.10 = (bf16[1024,512]{1,0:T(8,128)(2,1)S(1)}, bf16[1024,512]{1,0:T(8,128)(2,1)S(1)}, u32[]{:S(2)}, u32[]{:S(2)}) collective-permute-start(bf16[1024,512]{1,0:T(8,128)(2,1)S(1)} %pad_maximum_fusion), channel_id=1, source_target_pairs={{0,124},{4,0},{8,4},{12,8},{16,12},{20,16},{24,20},{28,24},{32,28}... | collective-permute-start | bytes 3145736 | tf_op jit(solution)/shard_map/ppermute | solution.py:381
  8.4 0.7 collective-permute-start.8
  9.1 0.1 pad_add_fusion.place
  9.2 9.7 %squares.1 = (f32[32,128]{1,0:T(8,128)S(1)}, f32[16,256,128]{2,1,0:T(8,128)S(1)}, f32[32,128]{1,0:T(8,128)S(1)}) custom-call(s32[3]{0:T(128)S(1)} %pad_add_fusion.place, f32[16,256]{1,0:T(8,128)S(1)} %copy-done.4, s32[16,256]{1,0:T(8,128)S(1)} %copy-done.5, f32[1,2048]{1,0:T(1,128)S(1)} %bitcast.18, f32[1,2048]{1,0:T(1,128)S(1)} %bitcast.20, ...), custom_call_target="tpu_custom_call" | custom-call | tf_op jit(solution)/shard_map/squares/pallas_call | solution.py:393
  18.9 0.0 copy-start
  18.9 1.3 copy-done
  20.2 0.5 collective-permute-done.8
  20.7 0.7 collective-permute-done
  21.4 0.8 collective-permute-start.3
  22.2 1.3 collective-permute-start.1
  23.4 1.7 %collective-permute-done.3 = f32[32,128]{1,0:T(8,128)S(1)} collective-permute-done((f32[32,128]{1,0:T(8,128)S(1)}, f32[32,128]{1,0:T(8,128)S(1)}, u32[]{:S(2)}, u32[]{:S(2)}) %collective-permute-start.3) | collective-permute-done | bytes 16416 | tf_op jit(solution)/shard_map/ppermute | solution.py:506
  25.1 2.3 %collective-permute-done.2 = f32[32,128]{1,0:T(8,128)S(1)} collective-permute-done((f32[32,128]{1,0:T(8,128)S(1)}, f32[32,128]{1,0:T(8,128)S(1)}, u32[]{:S(2)}, u32[]{:S(2)}) %collective-permute-start.2) | collective-permute-done | bytes 16416 | tf_op jit(solution)/shard_map/ppermute | solution.py:506
  27.4 0.4 collective-permute-done.1
  27.8 4.9 %collective-permute-start.6 = (f32[32,128]{1,0:T(8,128)S(1)}, f32[32,128]{1,0:T(8,128)S(1)}, u32[]{:S(2)}, u32[]{:S(2)}) collective-permute-start(f32[32,128]{1,0:T(8,128)S(1)} %add_add_fusion.squares_a), channel_id=1, source_target_pairs={{0,96},{4,100},{8,104},{12,108},{16,112},{20,116},{24,120},{28,124... | collective-permute-start | bytes 49160 | tf_op jit(solution)/shard_map/ppermute | solution.py:508
  32.7 0.9 collective-permute-start.4
  33.7 0.6 pad_maximum_fusion.3
  34.3 3.7 %collective-permute-done.5.squares_c = f32[32,128]{1,0:T(8,128)S(1)} collective-permute-done((f32[32,128]{1,0:T(8,128)S(1)}, f32[32,128]{1,0:T(8,128)S(1)}, u32[]{:S(2)}, u32[]{:S(2)}) %collective-permute-start.5) | collective-permute-done | bytes 16416 | tf_op jit(solution)/shard_map/ppermute | solution.py:508
  38.1 0.5 copy-done.13
  38.6 0.0 copy-done.14
  38.6 0.2 copy-done.10
  38.8 0.4 copy-done.9
  39.2 38.4 %form.1 = (bf16[16,256,2048]{2,1,0:T(8,128)(2,1)S(1)}, f32[16,72,128]{2,1,0:T(8,128)S(1)}, f32[16,72,128]{2,1,0:T(8,128)S(1)}) custom-call(s32[3]{0:T(128)} %copy-done.6, f32[16,256,128]{2,1,0:T(8,128)} %copy-done, f32[32,128]{1,0:T(8,128)} %copy-done.11, f32[32,128]{1,0:T(8,128)} %copy-done.14, f32[32,128]{1,0:T(8,128)} %copy-done.13, ...), custom_call_target="tpu_custom_call" | custom-call | tf_op jit(solution)/shard_map/form/pallas_call | solution.py:417
  77.6 0.1 collective-permute-start.11
  77.7 2.0 %collective-permute-done.11 = f32[16,72,128]{2,1,0:T(8,128)S(1)} collective-permute-done((f32[16,72,128]{2,1,0:T(8,128)S(1)}, f32[16,72,128]{2,1,0:T(8,128)S(1)}, u32[]{:S(2)}, u32[]{:S(2)}) %collective-permute-start.11) | collective-permute-done | bytes 589856 | tf_op jit(solution)/shard_map/ppermute | solution.py:460
  79.7 0.1 add.37
  79.8 17.2 %all_to_all.10.arrived = f32[16,72,128]{2,1,0:T(8,128)S(1)} all-to-all(f32[16,72,128]{2,1,0:T(8,128)S(1)} %add.37), channel_id=1, replica_groups={{0,8,16,24,32,40,48,56,64,72,80,88,96,104,112,120},{4,12,20,28,36,44,52..., dimensions={0} | all-to-all | bytes 1179648 | tf_op jit(solution)/shard_map/all_to_all | solution.py:460
  97.0 0.6 copy-done.7
  97.6 0.7 update.1
  98.2 14.6 %all_to_all.11.mine = f32[16,72,128]{2,1,0:T(8,128)S(1)} all-to-all(f32[16,72,128]{2,1,0:T(8,128)S(1)} %update.1), channel_id=1, replica_groups={{0,8,16,24,32,40,48,56,64,72,80,88,96,104,112,120},{4,12,20,28,36,44,52..., dimensions={0} | all-to-all | bytes 1179648 | tf_op jit(solution)/shard_map/all_to_all | solution.py:469
  112.9 2.0 %collective-permute-done.12.other = f32[16,72,128]{2,1,0:T(8,128)S(1)} collective-permute-done((f32[16,72,128]{2,1,0:T(8,128)S(1)}, f32[16,72,128]{2,1,0:T(8,128)S(1)}, u32[]{:S(2)}, u32[]{:S(2)}) %collective-permute-start.12) | collective-permute-done | bytes 589856 | tf_op jit(solution)/shard_map/ppermute | solution.py:470
  114.9 5.4 %refine.1 = (f32[16,64,2048]{2,1,0:T(8,128)S(1)}, f32[16,128]{1,0:T(8,128)S(1)}, f32[16,128]{1,0:T(8,128)}) custom-call(s32[3]{0:T(128)S(1)} %copy-done.8, f32[16,72,128]{2,1,0:T(8,128)S(1)} %all_to_all.11.mine, f32[16,72,128]{2,1,0:T(8,128)S(1)} %collective-permute-done.12.other, bf16[16,256,2048]{2,1,0:T(8,128)(2,1)S(1)} %get-tuple-element.16.formed), custom_call_target="tpu_custom_call" | custom-call | tf_op jit(solution)/shard_map/refine/pallas_call | solution.py:472
  120.3 0.1 collective-permute-start.13
  120.5 1.0 collective-permute-done.13
  121.5 1.2 collective-permute-start.16
  122.7 1.5 %collective-permute-start.15 = (f32[16,128]{1,0:T(8,128)S(1)}, f32[16,128]{1,0:T(8,128)S(1)}, u32[]{:S(2)}, u32[]{:S(2)}) collective-permute-start(f32[16,128]{1,0:T(8,128)S(1)} %add.38), channel_id=1, source_target_pairs={{0,16},{4,20},{8,24},{12,28},{16,0},{20,4},{24,8},{28,12},{32,48},... | collective-permute-start | bytes 24584 | tf_op jit(solution)/shard_map/ppermute | solution.py:506
  124.2 0.1 collective-permute-start.14
  124.3 0.9 collective-permute-done.16
  125.2 2.7 %collective-permute-done.15 = f32[16,128]{1,0:T(8,128)S(1)} collective-permute-done((f32[16,128]{1,0:T(8,128)S(1)}, f32[16,128]{1,0:T(8,128)S(1)}, u32[]{:S(2)}, u32[]{:S(2)}) %collective-permute-start.15) | collective-permute-done | bytes 8224 | tf_op jit(solution)/shard_map/ppermute | solution.py:506
  127.9 1.2 collective-permute-done.14
  129.1 1.1 collective-permute-start.19
  130.2 1.5 %collective-permute-start.18 = (f32[16,128]{1,0:T(8,128)S(1)}, f32[16,128]{1,0:T(8,128)S(1)}, u32[]{:S(2)}, u32[]{:S(2)}) collective-permute-start(f32[16,128]{1,0:T(8,128)S(1)} %add_add_fusion.1.sums_a), channel_id=1, source_target_pairs={{0,64},{4,68},{8,72},{12,76},{16,80},{20,84},{24,88},{28,92},{32,9... | collective-permute-start | bytes 24584 | tf_op jit(solution)/shard_map/ppermute | solution.py:508
  131.7 1.1 collective-permute-done.19.sums_d
  132.7 2.6 %collective-permute-done.18.sums_c = f32[16,128]{1,0:T(8,128)S(1)} collective-permute-done((f32[16,128]{1,0:T(8,128)S(1)}, f32[16,128]{1,0:T(8,128)S(1)}, u32[]{:S(2)}, u32[]{:S(2)}) %collective-permute-start.18) | collective-permute-done | bytes 8224 | tf_op jit(solution)/shard_map/ppermute | solution.py:508
  135.3 1.2 collective-permute-done.17.sums_b
  136.5 3.5 %scale.1 = f32[16,64,2048]{2,1,0:T(8,128)} custom-call(f32[16,128]{1,0:T(8,128)S(1)} %add_add_fusion.1.sums_a, f32[16,128]{1,0:T(8,128)S(1)} %collective-permute-done.17.sums_b, f32[16,128]{1,0:T(8,128)S(1)} %collective-permute-done.18.sums_c, f32[16,128]{1,0:T(8,128)S(1)} %collective-permute-done.19.sums_d, f32[16,64,2048]{2,1,0:T(8,128)S(1)} %get-tuple-element.18.updated), custom_call_target="tpu_custom_call" | custom-call | tf_op jit(solution)/shard_map/scale/pallas_call | solution.py:484
  (42 shorter events, 0.1 us)
Async XLA Ops:
  0.6 7.7 %copy-start.3 = (s32[2048]{0:T(1024)S(1)}, s32[2048]{0:T(1024)}, u32[]{:S(2)}) copy-start(s32[2048]{0:T(1024)} %param.11) | copy-start | bytes 24580
  0.6 7.7 %copy-start.2 = (f32[2048]{0:T(1024)S(1)}, f32[2048]{0:T(1024)}, u32[]{:S(2)}) copy-start(f32[2048]{0:T(1024)} %param.10) | copy-start | bytes 24580
  0.7 7.7 %copy-start.1 = (f32[2048]{0:T(1024)S(1)}, f32[2048]{0:T(1024)}, u32[]{:S(2)}) copy-start(f32[2048]{0:T(1024)} %param.9) | copy-start | bytes 24580
  0.7 8.5 %copy-start.5 = (s32[16,256]{1,0:T(8,128)S(1)}, s32[16,256]{1,0:T(8,128)}, u32[]{:S(2)}) copy-start(s32[16,256]{1,0:T(8,128)} %order_hbm.1) | copy-start | bytes 49156
  0.7 8.5 %copy-start.4 = (f32[16,256]{1,0:T(8,128)S(1)}, f32[16,256]{1,0:T(8,128)}, u32[]{:S(2)}) copy-start(f32[16,256]{1,0:T(8,128)} %roots_hbm.1) | copy-start | bytes 49156
  2.5 35.5 %collective-permute-start.10 = (bf16[1024,512]{1,0:T(8,128)(2,1)S(1)}, bf16[1024,512]{1,0:T(8,128)(2,1)S(1)}, u32[]{:S(2)}, u32[]{:S(2)}) collective-permute-start(bf16[1024,512]{1,0:T(8,128)(2,1)S(1)} %pad_maximum_fusion), channel_id=1, source_target_pairs={{0,124},{4,0},{8,4},{12,8},{16,12},{20,16},{24,20},{28,24},{32,28}... | collective-permute-start | bytes 3145736 | tf_op jit(solution)/shard_map/ppermute | solution.py:381
  8.4 12.3 %collective-permute-start.8 = (f32[2,512]{1,0:T(2,128)S(1)}, f32[2,512]{1,0:T(2,128)S(1)}, u32[]{:S(2)}, u32[]{:S(2)}) collective-permute-start(f32[2,512]{1,0:T(2,128)S(1)} %get-tuple-element.22), channel_id=1, source_target_pairs={{0,124},{4,0},{8,4},{12,8},{16,12},{20,16},{24,20},{28,24},{32,28}... | collective-permute-start | bytes 12296 | tf_op jit(solution)/shard_map/ppermute | solution.py:386
  9.1 13.1 %collective-permute-start.7 = (f32[2,512]{1,0:T(2,128)S(1)}, f32[2,512]{1,0:T(2,128)S(1)}, u32[]{:S(2)}, u32[]{:S(2)}) collective-permute-start(f32[2,512]{1,0:T(2,128)S(1)} %get-tuple-element.23), channel_id=1, source_target_pairs={{0,4},{4,8},{8,12},{12,16},{16,20},{20,24},{24,28},{28,32},{32,36}... | collective-permute-start | bytes 12296 | tf_op jit(solution)/shard_map/ppermute | solution.py:385
  9.1 28.9 %collective-permute-start.9 = (bf16[512,512]{1,0:T(8,128)(2,1)S(1)}, bf16[512,512]{1,0:T(8,128)(2,1)S(1)}, u32[]{:S(2)}, u32[]{:S(2)}) collective-permute-start(bf16[512,512]{1,0:T(8,128)(2,1)S(1)} %get-tuple-element.21), channel_id=1, source_target_pairs={{0,4},{4,8},{8,12},{12,16},{16,20},{20,24},{24,28},{28,32},{32,36}... | collective-permute-start | bytes 1572872 | tf_op jit(solution)/shard_map/ppermute | solution.py:380
  9.2 28.8 %copy-start.6 = (s32[3]{0:T(128)}, s32[3]{0:T(128)S(1)}, u32[]{:S(2)}) copy-start(s32[3]{0:T(128)S(1)} %pad_add_fusion.place) | copy-start | bytes 40
  18.9 1.3 copy-start
  20.2 1.2 collective-permute-start
  21.4 3.7 %collective-permute-start.3 = (f32[32,128]{1,0:T(8,128)S(1)}, f32[32,128]{1,0:T(8,128)S(1)}, u32[]{:S(2)}, u32[]{:S(2)}) collective-permute-start(f32[32,128]{1,0:T(8,128)S(1)} %add.33), channel_id=1, source_target_pairs={{0,24},{4,28},{8,0},{12,4},{16,8},{20,12},{24,16},{28,20},{32,56},... | collective-permute-start | bytes 49160 | tf_op jit(solution)/shard_map/ppermute | solution.py:506
  22.2 5.2 %collective-permute-start.2 = (f32[32,128]{1,0:T(8,128)S(1)}, f32[32,128]{1,0:T(8,128)S(1)}, u32[]{:S(2)}, u32[]{:S(2)}) collective-permute-start(f32[32,128]{1,0:T(8,128)S(1)} %add.33), channel_id=1, source_target_pairs={{0,16},{4,20},{8,24},{12,28},{16,0},{20,4},{24,8},{28,12},{32,48},... | collective-permute-start | bytes 49160 | tf_op jit(solution)/shard_map/ppermute | solution.py:506
  22.2 5.6 %collective-permute-start.1 = (f32[32,128]{1,0:T(8,128)S(1)}, f32[32,128]{1,0:T(8,128)S(1)}, u32[]{:S(2)}, u32[]{:S(2)}) collective-permute-start(f32[32,128]{1,0:T(8,128)S(1)} %add.33), channel_id=1, source_target_pairs={{0,8},{4,12},{8,16},{12,20},{16,24},{20,28},{24,0},{28,4},{32,40},... | collective-permute-start | bytes 49160 | tf_op jit(solution)/shard_map/ppermute | solution.py:506
  27.8 10.2 %copy-start.11 = (f32[32,128]{1,0:T(8,128)}, f32[32,128]{1,0:T(8,128)S(1)}, u32[]{:S(2)}) copy-start(f32[32,128]{1,0:T(8,128)S(1)} %add_add_fusion.squares_a) | copy-start | bytes 49156
  27.8 6.5 %collective-permute-start.6 = (f32[32,128]{1,0:T(8,128)S(1)}, f32[32,128]{1,0:T(8,128)S(1)}, u32[]{:S(2)}, u32[]{:S(2)}) collective-permute-start(f32[32,128]{1,0:T(8,128)S(1)} %add_add_fusion.squares_a), channel_id=1, source_target_pairs={{0,96},{4,100},{8,104},{12,108},{16,112},{20,116},{24,120},{28,124... | collective-permute-start | bytes 49160 | tf_op jit(solution)/shard_map/ppermute | solution.py:508
  32.7 5.2 %collective-permute-start.5 = (f32[32,128]{1,0:T(8,128)S(1)}, f32[32,128]{1,0:T(8,128)S(1)}, u32[]{:S(2)}, u32[]{:S(2)}) collective-permute-start(f32[32,128]{1,0:T(8,128)S(1)} %add_add_fusion.squares_a), channel_id=1, source_target_pairs={{0,64},{4,68},{8,72},{12,76},{16,80},{20,84},{24,88},{28,92},{32,9... | collective-permute-start | bytes 49160 | tf_op jit(solution)/shard_map/ppermute | solution.py:508
  32.7 5.2 %collective-permute-start.4 = (f32[32,128]{1,0:T(8,128)S(1)}, f32[32,128]{1,0:T(8,128)S(1)}, u32[]{:S(2)}, u32[]{:S(2)}) collective-permute-start(f32[32,128]{1,0:T(8,128)S(1)} %add_add_fusion.squares_a), channel_id=1, source_target_pairs={{0,32},{4,36},{8,40},{12,44},{16,48},{20,52},{24,56},{28,60},{32,6... | collective-permute-start | bytes 49160 | tf_op jit(solution)/shard_map/ppermute | solution.py:508
  34.3 3.8 %copy-start.12 = (f32[32,128]{1,0:T(8,128)}, f32[32,128]{1,0:T(8,128)S(1)}, u32[]{:S(2)}) copy-start(f32[32,128]{1,0:T(8,128)S(1)} %collective-permute-done.6.squares_d) | copy-start | bytes 49156
  38.0 0.6 copy-start.13
  38.0 0.6 copy-start.14
  38.0 0.8 copy-start.10
  38.0 1.1 copy-start.9
  77.6 37.3 %copy-start.8 = (s32[3]{0:T(128)S(1)}, s32[3]{0:T(128)}, u32[]{:S(2)}) copy-start(s32[3]{0:T(128)} %copy-done.6) | copy-start | bytes 40
  77.6 2.1 %collective-permute-start.11 = (f32[16,72,128]{2,1,0:T(8,128)S(1)}, f32[16,72,128]{2,1,0:T(8,128)S(1)}, u32[]{:S(2)}, u32[]{:S(2)}) collective-permute-start(f32[16,72,128]{2,1,0:T(8,128)S(1)} %get-tuple-element.14), channel_id=1, source_target_pairs={{0,4},{4,0},{8,12},{12,8},{16,20},{20,16},{24,28},{28,24},{32,36},... | collective-permute-start | bytes 1769480 | tf_op jit(solution)/shard_map/ppermute | solution.py:460
  97.0 0.6 copy-start.7
  112.9 2.0 %collective-permute-start.12 = (f32[16,72,128]{2,1,0:T(8,128)S(1)}, f32[16,72,128]{2,1,0:T(8,128)S(1)}, u32[]{:S(2)}, u32[]{:S(2)}) collective-permute-start(f32[16,72,128]{2,1,0:T(8,128)S(1)} %all_to_all.11.mine), channel_id=1, source_target_pairs={{0,4},{4,0},{8,12},{12,8},{16,20},{20,16},{24,28},{28,24},{32,36},... | collective-permute-start | bytes 1769480 | tf_op jit(solution)/shard_map/ppermute | solution.py:470
  120.3 1.2 collective-permute-start.13
  121.5 3.7 %collective-permute-start.16 = (f32[16,128]{1,0:T(8,128)S(1)}, f32[16,128]{1,0:T(8,128)S(1)}, u32[]{:S(2)}, u32[]{:S(2)}) collective-permute-start(f32[16,128]{1,0:T(8,128)S(1)} %add.38), channel_id=1, source_target_pairs={{0,24},{4,28},{8,0},{12,4},{16,8},{20,12},{24,16},{28,20},{32,56},... | collective-permute-start | bytes 24584 | tf_op jit(solution)/shard_map/ppermute | solution.py:506
  122.7 5.2 %collective-permute-start.15 = (f32[16,128]{1,0:T(8,128)S(1)}, f32[16,128]{1,0:T(8,128)S(1)}, u32[]{:S(2)}, u32[]{:S(2)}) collective-permute-start(f32[16,128]{1,0:T(8,128)S(1)} %add.38), channel_id=1, source_target_pairs={{0,16},{4,20},{8,24},{12,28},{16,0},{20,4},{24,8},{28,12},{32,48},... | collective-permute-start | bytes 24584 | tf_op jit(solution)/shard_map/ppermute | solution.py:506
  124.2 4.9 %collective-permute-start.14 = (f32[16,128]{1,0:T(8,128)S(1)}, f32[16,128]{1,0:T(8,128)S(1)}, u32[]{:S(2)}, u32[]{:S(2)}) collective-permute-start(f32[16,128]{1,0:T(8,128)S(1)} %add.38), channel_id=1, source_target_pairs={{0,8},{4,12},{8,16},{12,20},{16,24},{20,28},{24,0},{28,4},{32,40},... | collective-permute-start | bytes 24584 | tf_op jit(solution)/shard_map/ppermute | solution.py:506
  129.1 3.7 %collective-permute-start.19 = (f32[16,128]{1,0:T(8,128)S(1)}, f32[16,128]{1,0:T(8,128)S(1)}, u32[]{:S(2)}, u32[]{:S(2)}) collective-permute-start(f32[16,128]{1,0:T(8,128)S(1)} %add_add_fusion.1.sums_a), channel_id=1, source_target_pairs={{0,96},{4,100},{8,104},{12,108},{16,112},{20,116},{24,120},{28,124... | collective-permute-start | bytes 24584 | tf_op jit(solution)/shard_map/ppermute | solution.py:508
  130.2 5.2 %collective-permute-start.18 = (f32[16,128]{1,0:T(8,128)S(1)}, f32[16,128]{1,0:T(8,128)S(1)}, u32[]{:S(2)}, u32[]{:S(2)}) collective-permute-start(f32[16,128]{1,0:T(8,128)S(1)} %add_add_fusion.1.sums_a), channel_id=1, source_target_pairs={{0,64},{4,68},{8,72},{12,76},{16,80},{20,84},{24,88},{28,92},{32,9... | collective-permute-start | bytes 24584 | tf_op jit(solution)/shard_map/ppermute | solution.py:508
  131.7 4.9 %collective-permute-start.17 = (f32[16,128]{1,0:T(8,128)S(1)}, f32[16,128]{1,0:T(8,128)S(1)}, u32[]{:S(2)}, u32[]{:S(2)}) collective-permute-start(f32[16,128]{1,0:T(8,128)S(1)} %add_add_fusion.1.sums_a), channel_id=1, source_target_pairs={{0,32},{4,36},{8,40},{12,44},{16,48},{20,52},{24,56},{28,60},{32,6... | collective-permute-start | bytes 24584 | tf_op jit(solution)/shard_map/ppermute | solution.py:508

commit v2 on v1

--- a/solution.py
+++ b/solution.py
@@ -14,6 +14,7 @@
 NT = (((1,), (1,)), ((), ()))
 NN = (((1,), (0,)), ((), ()))
 LANES = 128
+WIDE = 256
 MIB = 1 << 20
 
 
@@ -27,6 +28,10 @@
 
 def column_of(row):
     return jnp.transpose(jnp.broadcast_to(row, (LANES, row.shape[1])))
+
+
+def twice(column):
+    return jnp.concatenate([column, column], axis=1)
 
 
 def row_of(column):
@@ -50,7 +55,7 @@
 
 
 def squares_body(
-    place, roots_hbm, order_hbm, poles_hbm, rank_hbm, deflated_hbm, chosen_out, columns_out, squares_out,
+    roots_hbm, order_hbm, poles_hbm, rank_hbm, deflated_hbm, chosen_out, squares_out,
     roots, order, poles, rank, deflated, weights, picked, sems,
 ):
     panels, size = roots.shape
@@ -63,7 +68,7 @@
         copy.wait()
     weights[...] = rank[...] * (1 - deflated[...]).astype(F32)
     slots = lax.broadcasted_iota(jnp.int32, (size, size), 1)
-    offset = place[0] * own
+    offset = lax.axis_index("col") * own
 
     def pick(p, slot):
         wanted = column_of(order[pl.ds(p, 1), :].astype(F32)).astype(jnp.int32)
@@ -77,7 +82,6 @@
         for quarter in range(4):
             start = pl.multiple_of((offset + quarter * own) % size, own)
             here = picked[slot, pl.ds(start, own), :]
-            columns_out[p, quarter * own : (quarter + 1) * own, :] = here
             total = jnp.zeros((own, LANES), F32)
             for k in range(rows // LANES):
                 lanes = pl.ds(k * LANES, LANES)
@@ -101,17 +105,19 @@
 
 
 def form_body(
-    place, columns, squares_a, squares_b, squares_c, squares_d, poles_hbm, rank_hbm, deflated_hbm, onsite_hbm,
+    chosen, squares_a, squares_b, squares_c, squares_d, poles_hbm, rank_hbm, deflated_hbm, onsite_hbm,
     pair_before, pair_after, q_hbm, before_hbm, after_hbm, diag_hbm, coup_hbm,
     formed, kept, sent,
-    staged, edge_formed, operated, acc, factors, squares, diag, coup, q, before, after, sym_parts, coup_parts,
+    staged, edge_formed, operated, acc, roots, own_roots, factors, squares, diag, coup, q, before, after, sym_parts, coup_parts,
     poles, rank, deflated, weights, onsite, grams, sems,
 ):
     panels, size = formed.shape[:2]
     count, block = q.shape[:2]
     own = size // 4
     chunks = block // LANES
-    core = place[1]
+    row = lax.axis_index("row")
+    core = row % 2
+    row_count = lax.axis_size("row")
     copies = fetch(
         [
             (poles_hbm, poles), (rank_hbm, rank), (deflated_hbm, deflated), (onsite_hbm, onsite),
@@ -126,42 +132,46 @@
 
     def prepare(p, slot):
         factors[slot] = column_of(lax.rsqrt(joined(squares, p) + EPSILON))
-
-    def evaluate(p, slot):
-        lam = columns[p]
-        factor = factors[slot]
-        for k in range(count * chunks):
-            lanes = slice(k * LANES, (k + 1) * LANES)
+        lam = column_of(joined(chosen, p))
+        roots[slot] = lam
+        own_roots[p] = lam[:own]
+
+    def evaluate(p, slot, b):
+        lam = twice(roots[slot])
+        factor = twice(factors[slot])
+        for k in range(chunks // 2):
+            lanes = slice(b * block + k * WIDE, b * block + (k + 1) * WIDE)
             cauchy = weights[:, lanes] * inverse(poles[:, lanes] - lam)
             staged[slot, :, lanes] = (cauchy * factor).astype(BF16)
-        for side, pair in enumerate((pair_before, pair_after)):
-            for k in range(chunks):
-                lanes = slice(k * LANES, (k + 1) * LANES)
-                cauchy = pair[1:2, lanes] * inverse(pair[0:1, lanes] - lam[:own])
-                operated[p, side * own : (side + 1) * own, lanes] = (cauchy * factor[:own]).astype(BF16)
-
-    def multiply(p, slot):
-        for b in range(count):
-            lanes = slice(b * block, (b + 1) * block)
-            formed[p, :, lanes] = dot(staged[slot, :, lanes], q[b], NT).astype(BF16)
+        if b < 2:
+            pair, missing = ((pair_before, row == 0), (pair_after, row == row_count - 1))[b]
+            near = jnp.where(missing, 0.0, 1.0)
+            for k in range(chunks // 2):
+                lanes = slice(k * WIDE, (k + 1) * WIDE)
+                cauchy = (near * pair[1:2, lanes]) * inverse(pair[0:1, lanes] - lam[:own])
+                operated[p, b * own : (b + 1) * own, lanes] = (cauchy * factor[:own]).astype(BF16)
+
+    def multiply(p, slot, b):
+        lanes = slice(b * block, (b + 1) * block)
+        formed[p, :, lanes] = dot(staged[slot, :, lanes], q[b], NT).astype(BF16)
 
     last = panels - 1
 
-    def two(i, carry):
-        p = 2 * i
-        multiply(p, 0)
-        evaluate(p + 1, 1)
-        prepare(jnp.minimum(p + 2, last), 0)
-        multiply(p + 1, 1)
-        evaluate(jnp.minimum(p + 2, last), 0)
-        prepare(jnp.minimum(p + 3, last), 1)
+    def four(i, carry):
+        for n in range(4):
+            p = 4 * i + n
+            for b in range(count):
+                multiply(p, n % 2, b)
+                evaluate(jnp.minimum(p + 1, last), 1 - n % 2, b)
+            prepare(jnp.minimum(p + 2, last), n % 2)
         return carry
 
     prepare(0, 0)
     prepare(1, 1)
-    evaluate(0, 0)
+    for b in range(count):
+        evaluate(0, 0, b)
     copies[4].wait()
-    lax.fori_loop(0, panels // 2, two, 0)
+    lax.fori_loop(0, panels // 4, four, 0)
     for copy in copies[5:]:
         copy.wait()
     for side, blocks in ((0, before[...]), (1, after[:block])):
@@ -218,13 +228,15 @@
     def finish(b):
         for p in range(panels):
             at = slice(p * own, (p + 1) * own)
-            lam = columns[p, :own]
+            lam = twice(own_roots[p])
             g = None if b == 0 else grams[at]
-            for k in range(chunks):
-                lanes = slice(b * block + k * LANES, b * block + (k + 1) * LANES)
+            for k in range(chunks // 2):
+                lanes = slice(b * block + k * WIDE, b * block + (k + 1) * WIDE)
                 f = formed[p, :own, lanes].astype(F32)
-                high, low = split(acc[b % 2, at, k * LANES : (k + 1) * LANES] - lam * f)
-                g = f * f if g is None else g + f * f
+                high, low = split(acc[b % 2, at, k * WIDE : (k + 1) * WIDE] - lam * f)
+                square = f * f
+                square = square[:, :LANES] + square[:, LANES:]
+                g = square if g is None else g + square
                 operated[p, :own, lanes] = high
                 operated[p, own:, lanes] = low
             grams[at] = g
@@ -257,24 +269,25 @@
         kept[p] = jnp.where(first, parts[0], parts[1])
         sent[p] = jnp.where(first, parts[1], parts[0])
 
-    def project_two(i, carry):
-        project(2 * i)
-        project(2 * i + 1)
+    def project_four(i, carry):
+        for n in range(4):
+            project(4 * i + n)
         return carry
 
-    lax.fori_loop(0, panels // 2, project_two, 0)
-
-
-def update_body(place, arrived, chosen, sent):
+    lax.fori_loop(0, panels // 4, project_four, 0)
+
+
+def update_body(arrived, chosen, sent):
     total = arrived[0]
     for n in range(1, arrived.shape[0]):
         total = total + arrived[n]
-    p = place[2]
+    p = lax.axis_index("row") // 2
+    core = lax.axis_index("row") % 2
     half = (total.shape[0] - 8) // 2
-    first = place[1] * half
+    first = core * half
     lam = joined(chosen, p)
     right = column_of(lam)
-    right = jnp.where(place[1] == 0, right[:half], right[half : 2 * half])
+    right = jnp.where(core == 0, right[:half], right[half : 2 * half])
     line = lax.broadcasted_iota(jnp.int32, (half, LANES), 0) + first
     lane = lax.broadcasted_iota(jnp.int32, (half, LANES), 1)
     same = line == lane
@@ -290,11 +303,11 @@
         sent[n] = made
 
 
-def refine_body(place, mine, other, formed, updated, sums, roots):
+def refine_body(mine, other, formed, updated, sums, roots):
     panels, size = formed.shape[:2]
     own = size // 4
     half = own // 2
-    zero = place[1] == 0
+    zero = lax.axis_index("row") % 2 == 0
 
     def panel(p):
         a, b = mine[p], other[p]
@@ -352,12 +365,12 @@
     return pl.BlockSpec(memory_space=pltpu.VMEM)
 
 
-def smem():
-    return pl.BlockSpec(memory_space=pltpu.SMEM)
-
-
 def hbm():
     return pl.BlockSpec(memory_space=pltpu.HBM)
+
+
+def anywhere():
+    return pl.BlockSpec(memory_space=pl.ANY)
 
 
 def shards(
@@ -370,9 +383,6 @@
     own = size // lax.axis_size("col")
     row_count = lax.axis_size("row")
     chips = row_count // 2
-    row = lax.axis_index("row")
-    place = jnp.stack([lax.axis_index("col"), row % 2, row // 2]).astype(jnp.int32)
-
     forward = [(i, (i + 1) % row_count) for i in range(row_count)]
     backward = [(i, (i - 1) % row_count) for i in range(row_count)]
     weights = rank_one * (1 - deflated).astype(F32)
@@ -381,24 +391,18 @@
     after = lax.ppermute(
         jnp.concatenate([q_blocks[0], coupling_blocks[0].astype(BF16)], axis=0), "row", backward
     )
-    ends = jnp.stack([row == 0, row == row_count - 1])
     pair_before = lax.ppermute(pair[:, rows - block :], "row", forward)
     pair_after = lax.ppermute(pair[:, :block], "row", backward)
-    pair_before, pair_after = (
-        jnp.stack([near[0], jnp.where(end, 0.0, near[1])])
-        for near, end in ((pair_before, ends[0]), (pair_after, ends[1]))
-    )
     vectors = (pole_values[None], rank_one[None], deflated[None])
 
-    chosen, columns, squares = pl.pallas_call(
+    chosen, squares = pl.pallas_call(
         squares_body,
         out_shape=[
             pltpu.VMEM((2 * panels, LANES), F32),
-            pltpu.VMEM((panels, size, LANES), F32),
             pltpu.VMEM((2 * panels, LANES), F32),
         ],
-        in_specs=[smem()] + [hbm()] * 5,
-        out_specs=[vmem()] * 3,
+        in_specs=[hbm()] * 5,
+        out_specs=[vmem()] * 2,
         scratch_shapes=[
             pltpu.VMEM((panels, size), F32),
             pltpu.VMEM((panels, size), jnp.int32),
@@ -411,7 +415,7 @@
         ],
         compiler_params=pltpu.CompilerParams(vmem_limit_bytes=8 * MIB),
         name="squares",
-    )(place, secular_roots, column_order, *vectors)
+    )(secular_roots, column_order, *vectors)
 
     depth = own + 8
     formed, kept, sent = pl.pallas_call(
@@ -421,13 +425,15 @@
             pltpu.VMEM((panels, depth, LANES), F32),
             pltpu.VMEM((panels, depth, LANES), F32),
         ],
-        in_specs=[smem()] + [vmem()] * 5 + [hbm()] * 4 + [vmem()] * 2 + [hbm()] * 5,
+        in_specs=[vmem()] * 5 + [hbm()] * 4 + [vmem()] * 2 + [hbm()] + [anywhere()] * 2 + [hbm()] * 2,
         out_specs=[vmem()] * 3,
         scratch_shapes=[
             pltpu.VMEM((2, size, rows), BF16),
             pltpu.VMEM((2, panels * own, block), BF16),
             pltpu.VMEM((panels, 2 * own, rows), BF16),
             pltpu.VMEM((2, panels * own, block), F32),
+            pltpu.VMEM((2, size, LANES), F32),
+            pltpu.VMEM((panels, own, LANES), F32),
             pltpu.VMEM((2, size, LANES), F32),
             pltpu.VMEM((2 * panels, LANES), F32),
             pltpu.VMEM((count, block, block), F32),
@@ -445,10 +451,10 @@
             pltpu.VMEM((panels * own, LANES), F32),
             pltpu.SemaphoreType.DMA((9,)),
         ],
-        compiler_params=pltpu.CompilerParams(vmem_limit_bytes=42 * MIB),
+        compiler_params=pltpu.CompilerParams(vmem_limit_bytes=38 * MIB),
         name="form",
     )(
-        place, columns, *over_rows(squares), *vectors, onsite_energy[None], pair_before, pair_after,
+        chosen, *over_rows(squares), *vectors, onsite_energy[None], pair_before, pair_after,
         q_blocks, before, after, diag_blocks, coupling_blocks,
     )
 
@@ -461,11 +467,11 @@
     shares = pl.pallas_call(
         update_body,
         out_shape=jax.ShapeDtypeStruct((chips, depth, LANES), F32),
-        in_specs=[smem()] + [vmem()] * 2,
+        in_specs=[vmem()] * 2,
         out_specs=vmem(),
         compiler_params=pltpu.CompilerParams(vmem_limit_bytes=8 * MIB),
         name="update",
-    )(place, arrived, chosen)
+    )(arrived, chosen)
     mine = spread(shares)
     other = lax.ppermute(mine, "row", swap)
 
@@ -476,11 +482,11 @@
             pltpu.VMEM((panels, LANES), F32),
             jax.ShapeDtypeStruct((panels, LANES), F32),
         ],
-        in_specs=[smem()] + [vmem()] * 3,
+        in_specs=[vmem()] * 3,
         out_specs=[vmem()] * 3,
         compiler_params=pltpu.CompilerParams(vmem_limit_bytes=12 * MIB),
         name="refine",
-    )(place, mine, other, formed)
+    )(mine, other, formed)
     refined = pl.pallas_call(
         functools.partial(scale_body, order=float(rows * row_count)),
         out_shape=jax.ShapeDtypeStruct((panels, own, rows), F32),

time: 140 us -> 135 us (0.964)
  Pallas kernels: 57.7 us -> 53.6 us
  waiting for transfers between devices: 23.9 us -> 26.8 us
  blocking collectives: 31.9 us -> 30.2 us
    ppermute x1, waiting for transfers between devices: 0.01 us -> 4.89 us  [shards(): pair_before = lax.ppermute(pair[:, rows - block:], 'row', forward)]
    ppermute x6, starting transfers between devices: 8.47 us -> 4.02 us  [over_rows(): return [value] + [lax.ppermute(value, 'row', move) for move in along_z]]
    ppermute x1, starting transfers between devices: 0.74 us -> 4.02 us  [shards(): pair_after = lax.ppermute(pair[:, :block], 'row', backward)]
    ppermute x6, waiting for transfers between devices: 9.15 us -> 6.47 us  [over_rows(): value = value + sum([lax.ppermute(value, 'row', move) for move in along_x])]
    pallas_call x1, Pallas kernels: 38.4 us -> 36 us  [shards(): pl.pallas_call(form_body, out_shape=[pltpu.VMEM((panels, size, rows), BF1...]
    all_to_all x1, blocking collectives: 17.2 us -> 15.4 us  [shards(): arrived = spread(kept + lax.ppermute(sent, 'row', swap))]
  transfers between devices with their start and end apart: 20 -> 20, of which waited for: 15 -> 14; matrix products, arithmetic and copies ran while one was open for 1% -> 0% of each run, Pallas kernels for 7% -> 7%
where the time goes in v2:
time: 135 us
  Pallas kernels  53.6 us (40%)
  blocking collectives  30.2 us (22%)
  waiting for transfers between devices  26.8 us (20%)
  starting transfers between devices  19.4 us (14%)
  local copies, waits for them, and re-layouts  3.42 us (3%)
    pallas_call x1, Pallas kernels, shards(): pl.pallas_call(form_body, out_shape=[pltpu.VMEM((panels, size, rows), BF1...  36 us
    all_to_all x1, blocking collectives, shards(): arrived = spread(kept + lax.ppermute(sent, 'row', swap))  15.4 us
    all_to_all x1, blocking collectives, shards(): mine = spread(shares)  14.8 us
    ppermute x6, waiting for transfers between devices, over_rows(): return [value] + [lax.ppermute(value, 'row', move) for move in along_z]  9.79 us
    pallas_call x1, Pallas kernels, shards(): pl.pallas_call(squares_body, out_shape=[pltpu.VMEM((2 * panels, LANES), F...  9.08 us
    ppermute x6, waiting for transfers between devices, over_rows(): value = value + sum([lax.ppermute(value, 'row', move) for move in along_x])  6.47 us
    ppermute x1, starting transfers between devices, shards(): lax.ppermute(jnp.concatenate([q_blocks[0], coupling_blocks[0].astype(BF16...  5.85 us
    ppermute x1, waiting for transfers between devices, shards(): pair_before = lax.ppermute(pair[:, rows - block:], 'row', forward)  4.89 us
  transfers between devices with their start and end apart: 20, of which 14 were waited for; matrix products, arithmetic and copies ran while one was open for 0% of the time, Pallas kernels for 7%

profile of v2, /device:TPU:0, one launch (start us, length us, event | category | flops | bytes accessed | tf_op | source)
XLA Modules:
  0.0 134.7 jit_solution(9879989716362746915)
XLA Ops:
  0.6 0.0 copy-start.2
  0.6 0.0 copy-start.1
  0.7 0.0 copy-start
  0.7 1.7 %slice_bitcast_fusion = (bf16[512,512]{1,0:T(8,128)(2,1)S(1)}, bf16[512,512]{1,0:T(8,128)(2,1)S(1)}, bf16[512,512]{1,0:T(8,128)(2,1)S(1)}) fusion(bf16[4,512,512]{2,1,0:T(8,128)(2,1)} %q_hbm.1, f32[4,512,512]{2,1,0:T(8,128)} %coup_hbm.1), kind=kLoop, calls=%fused_computation.3 | loop fusion | bytes 3145728 | tf_op jit(solution)/shard_map/squeeze | solution.py:392
  2.4 0.1 pad_maximum_fusion
  2.5 5.9 %collective-permute-start.10 = (bf16[1024,512]{1,0:T(8,128)(2,1)S(1)}, bf16[1024,512]{1,0:T(8,128)(2,1)S(1)}, u32[]{:S(2)}, u32[]{:S(2)}) collective-permute-start(bf16[1024,512]{1,0:T(8,128)(2,1)S(1)} %pad_maximum_fusion), channel_id=1, source_target_pairs={{0,124},{4,0},{8,4},{12,8},{16,12},{20,16},{24,20},{28,24},{32,28}... | collective-permute-start | bytes 3145736 | tf_op jit(solution)/shard_map/ppermute | solution.py:391
  8.3 9.1 %squares.1 = (f32[32,128]{1,0:T(8,128)S(1)}, f32[32,128]{1,0:T(8,128)S(1)}) custom-call(f32[16,256]{1,0:T(8,128)S(1)} %copy-done.5, s32[16,256]{1,0:T(8,128)S(1)} %copy-done.6, f32[1,2048]{1,0:T(1,128)S(1)} %bitcast.14, f32[1,2048]{1,0:T(1,128)S(1)} %bitcast.17, s32[1,2048]{1,0:T(1,128)S(1)} %bitcast.19), custom_call_target="tpu_custom_call" | custom-call | tf_op jit(solution)/shard_map/squares/pallas_call | solution.py:398
  17.4 0.6 copy-done.3
  18.0 0.0 collective-permute-start
  18.0 0.5 collective-permute-start.9
  18.6 0.7 collective-permute-done
  19.2 0.1 collective-permute-start.2
  19.3 1.9 %collective-permute-start.1 = (f32[32,128]{1,0:T(8,128)S(1)}, f32[32,128]{1,0:T(8,128)S(1)}, u32[]{:S(2)}, u32[]{:S(2)}) collective-permute-start(f32[32,128]{1,0:T(8,128)S(1)} %add.27), channel_id=1, source_target_pairs={{0,8},{4,12},{8,16},{12,20},{16,24},{20,28},{24,0},{28,4},{32,40},... | collective-permute-start | bytes 49160 | tf_op jit(solution)/shard_map/ppermute | solution.py:512
  21.3 1.7 %collective-permute-done.3 = f32[32,128]{1,0:T(8,128)S(1)} collective-permute-done((f32[32,128]{1,0:T(8,128)S(1)}, f32[32,128]{1,0:T(8,128)S(1)}, u32[]{:S(2)}, u32[]{:S(2)}) %collective-permute-start.3) | collective-permute-done | bytes 16416 | tf_op jit(solution)/shard_map/ppermute | solution.py:512
  23.0 4.0 %collective-permute-start.8 = (f32[2,512]{1,0:T(2,128)S(1)}, f32[2,512]{1,0:T(2,128)S(1)}, u32[]{:S(2)}, u32[]{:S(2)}) collective-permute-start(f32[2,512]{1,0:T(2,128)S(1)} %get-tuple-element.20), channel_id=1, source_target_pairs={{0,124},{4,0},{8,4},{12,8},{16,12},{20,16},{24,20},{28,24},{32,28}... | collective-permute-start | bytes 12296 | tf_op jit(solution)/shard_map/ppermute | solution.py:395
  27.0 0.0 collective-permute-done.2
  27.0 0.0 collective-permute-start.7
  27.0 1.4 %collective-permute-start.6 = (f32[32,128]{1,0:T(8,128)S(1)}, f32[32,128]{1,0:T(8,128)S(1)}, u32[]{:S(2)}, u32[]{:S(2)}) collective-permute-start(f32[32,128]{1,0:T(8,128)S(1)} %add_add_fusion.squares_a), channel_id=1, source_target_pairs={{0,96},{4,100},{8,104},{12,108},{16,112},{20,116},{24,120},{28,124... | collective-permute-start | bytes 49160 | tf_op jit(solution)/shard_map/ppermute | solution.py:514
  28.5 4.9 %collective-permute-done.7.pair_before = f32[2,512]{1,0:T(2,128)S(1)} collective-permute-done((f32[2,512]{1,0:T(2,128)S(1)}, f32[2,512]{1,0:T(2,128)S(1)}, u32[]{:S(2)}, u32[]{:S(2)}) %collective-permute-start.7) | collective-permute-done | bytes 4128 | tf_op jit(solution)/shard_map/ppermute | solution.py:394
  33.4 0.3 collective-permute-done.5.squares_c
  33.7 4.6 %collective-permute-done.4.squares_b = f32[32,128]{1,0:T(8,128)S(1)} collective-permute-done((f32[32,128]{1,0:T(8,128)S(1)}, f32[32,128]{1,0:T(8,128)S(1)}, u32[]{:S(2)}, u32[]{:S(2)}) %collective-permute-start.4) | collective-permute-done | bytes 16416 | tf_op jit(solution)/shard_map/ppermute | solution.py:514
  38.3 0.0 copy-start.7
  38.4 0.5 copy-done.12
  38.9 0.2 copy-done.8
  39.1 0.4 copy-done.7
  39.4 36.0 %form.1 = (bf16[16,256,2048]{2,1,0:T(8,128)(2,1)S(1)}, f32[16,72,128]{2,1,0:T(8,128)S(1)}, f32[16,72,128]{2,1,0:T(8,128)S(1)}) custom-call(f32[32,128]{1,0:T(8,128)} %copy-done.3, f32[32,128]{1,0:T(8,128)} %copy-done.9, f32[32,128]{1,0:T(8,128)} %copy-done.12, f32[32,128]{1,0:T(8,128)} %copy-done.11, f32[32,128]{1,0:T(8,128)} %copy-done.10, ...), custom_call_target="tpu_custom_call" | custom-call | tf_op jit(solution)/shard_map/form/pallas_call | solution.py:421
  75.4 0.1 collective-permute-start.11
  75.5 2.0 %collective-permute-done.11 = f32[16,72,128]{2,1,0:T(8,128)S(1)} collective-permute-done((f32[16,72,128]{2,1,0:T(8,128)S(1)}, f32[16,72,128]{2,1,0:T(8,128)S(1)}, u32[]{:S(2)}, u32[]{:S(2)}) %collective-permute-start.11) | collective-permute-done | bytes 589856 | tf_op jit(solution)/shard_map/ppermute | solution.py:466
  77.5 0.1 add.31
  77.6 15.4 %all_to_all.10.arrived = f32[16,72,128]{2,1,0:T(8,128)S(1)} all-to-all(f32[16,72,128]{2,1,0:T(8,128)S(1)} %add.31), channel_id=1, replica_groups={{0,8,16,24,32,40,48,56,64,72,80,88,96,104,112,120},{4,12,20,28,36,44,52..., dimensions={0} | all-to-all | bytes 1179648 | tf_op jit(solution)/shard_map/all_to_all | solution.py:466
  93.0 0.1 update.1
  93.1 14.8 %all_to_all.11.mine = f32[16,72,128]{2,1,0:T(8,128)S(1)} all-to-all(f32[16,72,128]{2,1,0:T(8,128)S(1)} %update.1), channel_id=1, replica_groups={{0,8,16,24,32,40,48,56,64,72,80,88,96,104,112,120},{4,12,20,28,36,44,52..., dimensions={0} | all-to-all | bytes 1179648 | tf_op jit(solution)/shard_map/all_to_all | solution.py:475
  107.9 2.0 %collective-permute-done.12.other = f32[16,72,128]{2,1,0:T(8,128)S(1)} collective-permute-done((f32[16,72,128]{2,1,0:T(8,128)S(1)}, f32[16,72,128]{2,1,0:T(8,128)S(1)}, u32[]{:S(2)}, u32[]{:S(2)}) %collective-permute-start.12) | collective-permute-done | bytes 589856 | tf_op jit(solution)/shard_map/ppermute | solution.py:476
  109.9 4.9 %refine.1 = (f32[16,64,2048]{2,1,0:T(8,128)S(1)}, f32[16,128]{1,0:T(8,128)S(1)}, f32[16,128]{1,0:T(8,128)}) custom-call(f32[16,72,128]{2,1,0:T(8,128)S(1)} %all_to_all.11.mine, f32[16,72,128]{2,1,0:T(8,128)S(1)} %collective-permute-done.12.other, bf16[16,256,2048]{2,1,0:T(8,128)(2,1)S(1)} %get-tuple-element.14.formed), custom_call_target="tpu_custom_call" | custom-call | tf_op jit(solution)/shard_map/refine/pallas_call | solution.py:478
  114.8 0.1 collective-permute-start.13
  115.0 1.0 collective-permute-done.13
  116.0 1.2 collective-permute-start.16
  117.2 1.5 %collective-permute-start.15 = (f32[16,128]{1,0:T(8,128)S(1)}, f32[16,128]{1,0:T(8,128)S(1)}, u32[]{:S(2)}, u32[]{:S(2)}) collective-permute-start(f32[16,128]{1,0:T(8,128)S(1)} %add.32), channel_id=1, source_target_pairs={{0,16},{4,20},{8,24},{12,28},{16,0},{20,4},{24,8},{28,12},{32,48},... | collective-permute-start | bytes 24584 | tf_op jit(solution)/shard_map/ppermute | solution.py:512
  118.7 0.1 collective-permute-start.14
  118.8 0.9 collective-permute-done.16
  119.6 2.7 %collective-permute-done.15 = f32[16,128]{1,0:T(8,128)S(1)} collective-permute-done((f32[16,128]{1,0:T(8,128)S(1)}, f32[16,128]{1,0:T(8,128)S(1)}, u32[]{:S(2)}, u32[]{:S(2)}) %collective-permute-start.15) | collective-permute-done | bytes 8224 | tf_op jit(solution)/shard_map/ppermute | solution.py:512
  122.3 1.2 collective-permute-done.14
  123.5 1.1 collective-permute-start.19
  124.7 1.5 %collective-permute-start.18 = (f32[16,128]{1,0:T(8,128)S(1)}, f32[16,128]{1,0:T(8,128)S(1)}, u32[]{:S(2)}, u32[]{:S(2)}) collective-permute-start(f32[16,128]{1,0:T(8,128)S(1)} %add_add_fusion.1.sums_a), channel_id=1, source_target_pairs={{0,64},{4,68},{8,72},{12,76},{16,80},{20,84},{24,88},{28,92},{32,9... | collective-permute-start | bytes 24584 | tf_op jit(solution)/shard_map/ppermute | solution.py:514
  126.1 1.1 collective-permute-done.19.sums_d
  127.2 2.6 %collective-permute-done.18.sums_c = f32[16,128]{1,0:T(8,128)S(1)} collective-permute-done((f32[16,128]{1,0:T(8,128)S(1)}, f32[16,128]{1,0:T(8,128)S(1)}, u32[]{:S(2)}, u32[]{:S(2)}) %collective-permute-start.18) | collective-permute-done | bytes 8224 | tf_op jit(solution)/shard_map/ppermute | solution.py:514
  129.8 1.2 collective-permute-done.17.sums_b
  131.0 3.5 %scale.1 = f32[16,64,2048]{2,1,0:T(8,128)} custom-call(f32[16,128]{1,0:T(8,128)S(1)} %add_add_fusion.1.sums_a, f32[16,128]{1,0:T(8,128)S(1)} %collective-permute-done.17.sums_b, f32[16,128]{1,0:T(8,128)S(1)} %collective-permute-done.18.sums_c, f32[16,128]{1,0:T(8,128)S(1)} %collective-permute-done.19.sums_d, f32[16,64,2048]{2,1,0:T(8,128)S(1)} %get-tuple-element.16.updated), custom_call_target="tpu_custom_call" | custom-call | tf_op jit(solution)/shard_map/scale/pallas_call | solution.py:490
  (38 shorter events, 0.1 us)
Async XLA Ops:
  0.6 7.7 %copy-start.2 = (s32[2048]{0:T(1024)S(1)}, s32[2048]{0:T(1024)}, u32[]{:S(2)}) copy-start(s32[2048]{0:T(1024)} %param.11) | copy-start | bytes 24580
  0.6 7.7 %copy-start.1 = (f32[2048]{0:T(1024)S(1)}, f32[2048]{0:T(1024)}, u32[]{:S(2)}) copy-start(f32[2048]{0:T(1024)} %param.10) | copy-start | bytes 24580
  0.7 7.7 %copy-start.6 = (s32[16,256]{1,0:T(8,128)S(1)}, s32[16,256]{1,0:T(8,128)}, u32[]{:S(2)}) copy-start(s32[16,256]{1,0:T(8,128)} %order_hbm.1) | copy-start | bytes 49156
  0.7 7.7 %copy-start.5 = (f32[16,256]{1,0:T(8,128)S(1)}, f32[16,256]{1,0:T(8,128)}, u32[]{:S(2)}) copy-start(f32[16,256]{1,0:T(8,128)} %roots_hbm.1) | copy-start | bytes 49156
  0.7 7.7 %copy-start = (f32[2048]{0:T(1024)S(1)}, f32[2048]{0:T(1024)}, u32[]{:S(2)}) copy-start(f32[2048]{0:T(1024)} %param.9) | copy-start | bytes 24580
  2.5 35.8 %collective-permute-start.10 = (bf16[1024,512]{1,0:T(8,128)(2,1)S(1)}, bf16[1024,512]{1,0:T(8,128)(2,1)S(1)}, u32[]{:S(2)}, u32[]{:S(2)}) collective-permute-start(bf16[1024,512]{1,0:T(8,128)(2,1)S(1)} %pad_maximum_fusion), channel_id=1, source_target_pairs={{0,124},{4,0},{8,4},{12,8},{16,12},{20,16},{24,20},{28,24},{32,28}... | collective-permute-start | bytes 3145736 | tf_op jit(solution)/shard_map/ppermute | solution.py:391
  17.4 0.6 copy-start.3
  18.0 1.2 collective-permute-start
  18.0 20.3 %collective-permute-start.9 = (bf16[512,512]{1,0:T(8,128)(2,1)S(1)}, bf16[512,512]{1,0:T(8,128)(2,1)S(1)}, u32[]{:S(2)}, u32[]{:S(2)}) collective-permute-start(bf16[512,512]{1,0:T(8,128)(2,1)S(1)} %get-tuple-element.19), channel_id=1, source_target_pairs={{0,4},{4,8},{8,12},{12,16},{16,20},{20,24},{24,28},{28,32},{32,36}... | collective-permute-start | bytes 1572872 | tf_op jit(solution)/shard_map/ppermute | solution.py:390
  19.2 3.7 %collective-permute-start.3 = (f32[32,128]{1,0:T(8,128)S(1)}, f32[32,128]{1,0:T(8,128)S(1)}, u32[]{:S(2)}, u32[]{:S(2)}) collective-permute-start(f32[32,128]{1,0:T(8,128)S(1)} %add.27), channel_id=1, source_target_pairs={{0,24},{4,28},{8,0},{12,4},{16,8},{20,12},{24,16},{28,20},{32,56},... | collective-permute-start | bytes 49160 | tf_op jit(solution)/shard_map/ppermute | solution.py:512
  19.2 7.8 %collective-permute-start.2 = (f32[32,128]{1,0:T(8,128)S(1)}, f32[32,128]{1,0:T(8,128)S(1)}, u32[]{:S(2)}, u32[]{:S(2)}) collective-permute-start(f32[32,128]{1,0:T(8,128)S(1)} %add.27), channel_id=1, source_target_pairs={{0,16},{4,20},{8,24},{12,28},{16,0},{20,4},{24,8},{28,12},{32,48},... | collective-permute-start | bytes 49160 | tf_op jit(solution)/shard_map/ppermute | solution.py:512
  19.3 7.7 %collective-permute-start.1 = (f32[32,128]{1,0:T(8,128)S(1)}, f32[32,128]{1,0:T(8,128)S(1)}, u32[]{:S(2)}, u32[]{:S(2)}) collective-permute-start(f32[32,128]{1,0:T(8,128)S(1)} %add.27), channel_id=1, source_target_pairs={{0,8},{4,12},{8,16},{12,20},{16,24},{20,28},{24,0},{28,4},{32,40},... | collective-permute-start | bytes 49160 | tf_op jit(solution)/shard_map/ppermute | solution.py:512
  23.0 5.5 %collective-permute-start.8 = (f32[2,512]{1,0:T(2,128)S(1)}, f32[2,512]{1,0:T(2,128)S(1)}, u32[]{:S(2)}, u32[]{:S(2)}) collective-permute-start(f32[2,512]{1,0:T(2,128)S(1)} %get-tuple-element.20), channel_id=1, source_target_pairs={{0,124},{4,0},{8,4},{12,8},{16,12},{20,16},{24,20},{28,24},{32,28}... | collective-permute-start | bytes 12296 | tf_op jit(solution)/shard_map/ppermute | solution.py:395
  27.0 6.4 %collective-permute-start.7 = (f32[2,512]{1,0:T(2,128)S(1)}, f32[2,512]{1,0:T(2,128)S(1)}, u32[]{:S(2)}, u32[]{:S(2)}) collective-permute-start(f32[2,512]{1,0:T(2,128)S(1)} %get-tuple-element.21), channel_id=1, source_target_pairs={{0,4},{4,8},{8,12},{12,16},{16,20},{20,24},{24,28},{28,32},{32,36}... | collective-permute-start | bytes 12296 | tf_op jit(solution)/shard_map/ppermute | solution.py:394
  27.0 11.3 %copy-start.9 = (f32[32,128]{1,0:T(8,128)}, f32[32,128]{1,0:T(8,128)S(1)}, u32[]{:S(2)}) copy-start(f32[32,128]{1,0:T(8,128)S(1)} %add_add_fusion.squares_a) | copy-start | bytes 49156
  27.0 6.3 %collective-permute-start.6 = (f32[32,128]{1,0:T(8,128)S(1)}, f32[32,128]{1,0:T(8,128)S(1)}, u32[]{:S(2)}, u32[]{:S(2)}) collective-permute-start(f32[32,128]{1,0:T(8,128)S(1)} %add_add_fusion.squares_a), channel_id=1, source_target_pairs={{0,96},{4,100},{8,104},{12,108},{16,112},{20,116},{24,120},{28,124... | collective-permute-start | bytes 49160 | tf_op jit(solution)/shard_map/ppermute | solution.py:514
  28.5 9.9 %copy-start.13 = (f32[2,512]{1,0:T(2,128)}, f32[2,512]{1,0:T(2,128)S(1)}, u32[]{:S(2)}) copy-start(f32[2,512]{1,0:T(2,128)S(1)} %collective-permute-done.8.pair_after) | copy-start | bytes 12292
  28.5 5.2 %collective-permute-start.5 = (f32[32,128]{1,0:T(8,128)S(1)}, f32[32,128]{1,0:T(8,128)S(1)}, u32[]{:S(2)}, u32[]{:S(2)}) collective-permute-start(f32[32,128]{1,0:T(8,128)S(1)} %add_add_fusion.squares_a), channel_id=1, source_target_pairs={{0,64},{4,68},{8,72},{12,76},{16,80},{20,84},{24,88},{28,92},{32,9... | collective-permute-start | bytes 49160 | tf_op jit(solution)/shard_map/ppermute | solution.py:514
  33.3 5.0 %copy-start.14 = (f32[2,512]{1,0:T(2,128)}, f32[2,512]{1,0:T(2,128)S(1)}, u32[]{:S(2)}) copy-start(f32[2,512]{1,0:T(2,128)S(1)} %collective-permute-done.7.pair_before) | copy-start | bytes 12292
  33.3 4.9 %collective-permute-start.4 = (f32[32,128]{1,0:T(8,128)S(1)}, f32[32,128]{1,0:T(8,128)S(1)}, u32[]{:S(2)}, u32[]{:S(2)}) collective-permute-start(f32[32,128]{1,0:T(8,128)S(1)} %add_add_fusion.squares_a), channel_id=1, source_target_pairs={{0,32},{4,36},{8,40},{12,44},{16,48},{20,52},{24,56},{28,60},{32,6... | collective-permute-start | bytes 49160 | tf_op jit(solution)/shard_map/ppermute | solution.py:514
  33.4 5.0 %copy-start.10 = (f32[32,128]{1,0:T(8,128)}, f32[32,128]{1,0:T(8,128)S(1)}, u32[]{:S(2)}) copy-start(f32[32,128]{1,0:T(8,128)S(1)} %collective-permute-done.6.squares_d) | copy-start | bytes 49156
  33.7 4.7 %copy-start.11 = (f32[32,128]{1,0:T(8,128)}, f32[32,128]{1,0:T(8,128)S(1)}, u32[]{:S(2)}) copy-start(f32[32,128]{1,0:T(8,128)S(1)} %collective-permute-done.5.squares_c) | copy-start | bytes 49156
  38.3 0.6 copy-start.12
  38.3 0.8 copy-start.8
  38.3 1.1 copy-start.7
  39.4 53.6 %copy-start.4 = (f32[32,128]{1,0:T(8,128)S(1)}, f32[32,128]{1,0:T(8,128)}, u32[]{:S(2)}) copy-start(f32[32,128]{1,0:T(8,128)} %copy-done.3) | copy-start | bytes 49156
  75.4 2.1 %collective-permute-start.11 = (f32[16,72,128]{2,1,0:T(8,128)S(1)}, f32[16,72,128]{2,1,0:T(8,128)S(1)}, u32[]{:S(2)}, u32[]{:S(2)}) collective-permute-start(f32[16,72,128]{2,1,0:T(8,128)S(1)} %get-tuple-element.13), channel_id=1, source_target_pairs={{0,4},{4,0},{8,12},{12,8},{16,20},{20,16},{24,28},{28,24},{32,36},... | collective-permute-start | bytes 1769480 | tf_op jit(solution)/shard_map/ppermute | solution.py:466
  107.9 2.0 %collective-permute-start.12 = (f32[16,72,128]{2,1,0:T(8,128)S(1)}, f32[16,72,128]{2,1,0:T(8,128)S(1)}, u32[]{:S(2)}, u32[]{:S(2)}) collective-permute-start(f32[16,72,128]{2,1,0:T(8,128)S(1)} %all_to_all.11.mine), channel_id=1, source_target_pairs={{0,4},{4,0},{8,12},{12,8},{16,20},{20,16},{24,28},{28,24},{32,36},... | collective-permute-start | bytes 1769480 | tf_op jit(solution)/shard_map/ppermute | solution.py:476
  114.8 1.2 collective-permute-start.13
  116.0 3.7 %collective-permute-start.16 = (f32[16,128]{1,0:T(8,128)S(1)}, f32[16,128]{1,0:T(8,128)S(1)}, u32[]{:S(2)}, u32[]{:S(2)}) collective-permute-start(f32[16,128]{1,0:T(8,128)S(1)} %add.32), channel_id=1, source_target_pairs={{0,24},{4,28},{8,0},{12,4},{16,8},{20,12},{24,16},{28,20},{32,56},... | collective-permute-start | bytes 24584 | tf_op jit(solution)/shard_map/ppermute | solution.py:512
  117.2 5.2 %collective-permute-start.15 = (f32[16,128]{1,0:T(8,128)S(1)}, f32[16,128]{1,0:T(8,128)S(1)}, u32[]{:S(2)}, u32[]{:S(2)}) collective-permute-start(f32[16,128]{1,0:T(8,128)S(1)} %add.32), channel_id=1, source_target_pairs={{0,16},{4,20},{8,24},{12,28},{16,0},{20,4},{24,8},{28,12},{32,48},... | collective-permute-start | bytes 24584 | tf_op jit(solution)/shard_map/ppermute | solution.py:512
  118.7 4.9 %collective-permute-start.14 = (f32[16,128]{1,0:T(8,128)S(1)}, f32[16,128]{1,0:T(8,128)S(1)}, u32[]{:S(2)}, u32[]{:S(2)}) collective-permute-start(f32[16,128]{1,0:T(8,128)S(1)} %add.32), channel_id=1, source_target_pairs={{0,8},{4,12},{8,16},{12,20},{16,24},{20,28},{24,0},{28,4},{32,40},... | collective-permute-start | bytes 24584 | tf_op jit(solution)/shard_map/ppermute | solution.py:512
  123.5 3.7 %collective-permute-start.19 = (f32[16,128]{1,0:T(8,128)S(1)}, f32[16,128]{1,0:T(8,128)S(1)}, u32[]{:S(2)}, u32[]{:S(2)}) collective-permute-start(f32[16,128]{1,0:T(8,128)S(1)} %add_add_fusion.1.sums_a), channel_id=1, source_target_pairs={{0,96},{4,100},{8,104},{12,108},{16,112},{20,116},{24,120},{28,124... | collective-permute-start | bytes 24584 | tf_op jit(solution)/shard_map/ppermute | solution.py:514
  124.7 5.2 %collective-permute-start.18 = (f32[16,128]{1,0:T(8,128)S(1)}, f32[16,128]{1,0:T(8,128)S(1)}, u32[]{:S(2)}, u32[]{:S(2)}) collective-permute-start(f32[16,128]{1,0:T(8,128)S(1)} %add_add_fusion.1.sums_a), channel_id=1, source_target_pairs={{0,64},{4,68},{8,72},{12,76},{16,80},{20,84},{24,88},{28,92},{32,9... | collective-permute-start | bytes 24584 | tf_op jit(solution)/shard_map/ppermute | solution.py:514
  126.1 4.9 %collective-permute-start.17 = (f32[16,128]{1,0:T(8,128)S(1)}, f32[16,128]{1,0:T(8,128)S(1)}, u32[]{:S(2)}, u32[]{:S(2)}) collective-permute-start(f32[16,128]{1,0:T(8,128)S(1)} %add_add_fusion.1.sums_a), channel_id=1, source_target_pairs={{0,32},{4,36},{8,40},{12,44},{16,48},{20,52},{24,56},{28,60},{32,6... | collective-permute-start | bytes 24584 | tf_op jit(solution)/shard_map/ppermute | solution.py:514

commit v3 on v2

--- a/solution.py
+++ b/solution.py
@@ -93,15 +93,14 @@
             chosen_out[pl.ds(2 * p + h, 1), :] = jnp.transpose(here)[0:1]
             squares_out[pl.ds(2 * p + h, 1), :] = row_of(total)
 
-    def two(i, carry):
-        pick(2 * i + 1, 1)
-        add_up(2 * i, 0)
-        pick(jnp.minimum(2 * i + 2, panels - 1), 0)
-        add_up(2 * i + 1, 1)
+    def four(i, carry):
+        for n in range(4):
+            pick(jnp.minimum(4 * i + n + 1, panels - 1), 1 - n % 2)
+            add_up(4 * i + n, n % 2)
         return carry
 
     pick(0, 0)
-    lax.fori_loop(0, panels // 2, two, 0)
+    lax.fori_loop(0, panels // 4, four, 0)
 
 
 def form_body(
@@ -330,12 +329,12 @@
         sums[pl.ds(p, 1), :] = row_of(jnp.concatenate([total, jnp.zeros_like(total)], axis=0))
         roots[pl.ds(p, 1), :] = low[own : own + 1] + high[own : own + 1]
 
-    def two(i, carry):
-        panel(2 * i)
-        panel(2 * i + 1)
+    def four(i, carry):
+        for n in range(4):
+            panel(4 * i + n)
         return carry
 
-    lax.fori_loop(0, panels // 2, two, 0)
+    lax.fori_loop(0, panels // 4, four, 0)
 
 
 def scale_body(sums_a, sums_b, sums_c, sums_d, updated, refined, sums, scaled, sems, *, order):

time: 135 us -> 134 us (level)
  no operation moved by 1% of the time
where the time goes in v3:
time: 134 us; the launch traced here: 133 us
  Pallas kernels  52.3 us (39%)
  blocking collectives  30.2 us (23%)
  waiting for transfers between devices  26.8 us (20%)
  starting transfers between devices  19.4 us (14%)
  local copies, waits for them, and re-layouts  3.42 us (3%)
    pallas_call x1, Pallas kernels, shards(): pl.pallas_call(form_body, out_shape=[pltpu.VMEM((panels, size, rows), BF1...  36 us
    all_to_all x1, blocking collectives, shards(): arrived = spread(kept + lax.ppermute(sent, 'row', swap))  15.4 us
    all_to_all x1, blocking collectives, shards(): mine = spread(shares)  14.8 us
    ppermute x6, waiting for transfers between devices, over_rows(): return [value] + [lax.ppermute(value, 'row', move) for move in along_z]  9.79 us
    pallas_call x1, Pallas kernels, shards(): pl.pallas_call(squares_body, out_shape=[pltpu.VMEM((2 * panels, LANES), F...  8.94 us
    ppermute x6, waiting for transfers between devices, over_rows(): value = value + sum([lax.ppermute(value, 'row', move) for move in along_x])  6.47 us
    ppermute x1, starting transfers between devices, shards(): lax.ppermute(jnp.concatenate([q_blocks[0], coupling_blocks[0].astype(BF16...  5.85 us
    ppermute x1, waiting for transfers between devices, shards(): pair_before = lax.ppermute(pair[:, rows - block:], 'row', forward)  4.89 us
  transfers between devices with their start and end apart: 20, of which 14 were waited for; matrix products, arithmetic and copies ran while one was open for 0% of the time, Pallas kernels for 7%

profile of v3, /device:TPU:0, one launch (start us, length us, event | category | flops | bytes accessed | tf_op | source)
XLA Modules:
  0.0 133.4 jit_solution(2778330093167098875)
XLA Ops:
  0.6 0.0 copy-start.2
  0.6 0.0 copy-start.1
  0.7 0.0 copy-start
  0.7 1.7 %slice_bitcast_fusion = (bf16[512,512]{1,0:T(8,128)(2,1)S(1)}, bf16[512,512]{1,0:T(8,128)(2,1)S(1)}, bf16[512,512]{1,0:T(8,128)(2,1)S(1)}) fusion(bf16[4,512,512]{2,1,0:T(8,128)(2,1)} %q_hbm.1, f32[4,512,512]{2,1,0:T(8,128)} %coup_hbm.1), kind=kLoop, calls=%fused_computation.3 | loop fusion | bytes 3145728 | tf_op jit(solution)/shard_map/squeeze | solution.py:391
  2.4 0.1 pad_maximum_fusion
  2.5 5.9 %collective-permute-start.10 = (bf16[1024,512]{1,0:T(8,128)(2,1)S(1)}, bf16[1024,512]{1,0:T(8,128)(2,1)S(1)}, u32[]{:S(2)}, u32[]{:S(2)}) collective-permute-start(bf16[1024,512]{1,0:T(8,128)(2,1)S(1)} %pad_maximum_fusion), channel_id=1, source_target_pairs={{0,124},{4,0},{8,4},{12,8},{16,12},{20,16},{24,20},{28,24},{32,28}... | collective-permute-start | bytes 3145736 | tf_op jit(solution)/shard_map/ppermute | solution.py:390
  8.3 8.9 %squares.1 = (f32[32,128]{1,0:T(8,128)S(1)}, f32[32,128]{1,0:T(8,128)S(1)}) custom-call(f32[16,256]{1,0:T(8,128)S(1)} %copy-done.5, s32[16,256]{1,0:T(8,128)S(1)} %copy-done.6, f32[1,2048]{1,0:T(1,128)S(1)} %bitcast.14, f32[1,2048]{1,0:T(1,128)S(1)} %bitcast.17, s32[1,2048]{1,0:T(1,128)S(1)} %bitcast.19), custom_call_target="tpu_custom_call" | custom-call | tf_op jit(solution)/shard_map/squares/pallas_call | solution.py:397
  17.3 0.6 copy-done.3
  17.9 0.0 collective-permute-start
  17.9 0.5 collective-permute-start.9
  18.4 0.7 collective-permute-done
  19.1 0.1 collective-permute-start.2
  19.2 1.9 %collective-permute-start.1 = (f32[32,128]{1,0:T(8,128)S(1)}, f32[32,128]{1,0:T(8,128)S(1)}, u32[]{:S(2)}, u32[]{:S(2)}) collective-permute-start(f32[32,128]{1,0:T(8,128)S(1)} %add.27), channel_id=1, source_target_pairs={{0,8},{4,12},{8,16},{12,20},{16,24},{20,28},{24,0},{28,4},{32,40},... | collective-permute-start | bytes 49160 | tf_op jit(solution)/shard_map/ppermute | solution.py:511
  21.1 1.7 %collective-permute-done.3 = f32[32,128]{1,0:T(8,128)S(1)} collective-permute-done((f32[32,128]{1,0:T(8,128)S(1)}, f32[32,128]{1,0:T(8,128)S(1)}, u32[]{:S(2)}, u32[]{:S(2)}) %collective-permute-start.3) | collective-permute-done | bytes 16416 | tf_op jit(solution)/shard_map/ppermute | solution.py:511
  22.8 4.0 %collective-permute-start.8 = (f32[2,512]{1,0:T(2,128)S(1)}, f32[2,512]{1,0:T(2,128)S(1)}, u32[]{:S(2)}, u32[]{:S(2)}) collective-permute-start(f32[2,512]{1,0:T(2,128)S(1)} %get-tuple-element.20), channel_id=1, source_target_pairs={{0,124},{4,0},{8,4},{12,8},{16,12},{20,16},{24,20},{28,24},{32,28}... | collective-permute-start | bytes 12296 | tf_op jit(solution)/shard_map/ppermute | solution.py:394
  26.9 0.0 collective-permute-done.2
  26.9 0.0 collective-permute-start.7
  26.9 1.4 %collective-permute-start.6 = (f32[32,128]{1,0:T(8,128)S(1)}, f32[32,128]{1,0:T(8,128)S(1)}, u32[]{:S(2)}, u32[]{:S(2)}) collective-permute-start(f32[32,128]{1,0:T(8,128)S(1)} %add_add_fusion.squares_a), channel_id=1, source_target_pairs={{0,96},{4,100},{8,104},{12,108},{16,112},{20,116},{24,120},{28,124... | collective-permute-start | bytes 49160 | tf_op jit(solution)/shard_map/ppermute | solution.py:513
  28.3 4.9 %collective-permute-done.7.pair_before = f32[2,512]{1,0:T(2,128)S(1)} collective-permute-done((f32[2,512]{1,0:T(2,128)S(1)}, f32[2,512]{1,0:T(2,128)S(1)}, u32[]{:S(2)}, u32[]{:S(2)}) %collective-permute-start.7) | collective-permute-done | bytes 4128 | tf_op jit(solution)/shard_map/ppermute | solution.py:393
  33.2 0.3 collective-permute-done.5.squares_c
  33.6 4.6 %collective-permute-done.4.squares_b = f32[32,128]{1,0:T(8,128)S(1)} collective-permute-done((f32[32,128]{1,0:T(8,128)S(1)}, f32[32,128]{1,0:T(8,128)S(1)}, u32[]{:S(2)}, u32[]{:S(2)}) %collective-permute-start.4) | collective-permute-done | bytes 16416 | tf_op jit(solution)/shard_map/ppermute | solution.py:513
  38.2 0.0 copy-start.7
  38.2 0.5 copy-done.12
  38.8 0.2 copy-done.8
  39.0 0.4 copy-done.7
  39.3 36.0 %form.1 = (bf16[16,256,2048]{2,1,0:T(8,128)(2,1)S(1)}, f32[16,72,128]{2,1,0:T(8,128)S(1)}, f32[16,72,128]{2,1,0:T(8,128)S(1)}) custom-call(f32[32,128]{1,0:T(8,128)} %copy-done.3, f32[32,128]{1,0:T(8,128)} %copy-done.9, f32[32,128]{1,0:T(8,128)} %copy-done.12, f32[32,128]{1,0:T(8,128)} %copy-done.11, f32[32,128]{1,0:T(8,128)} %copy-done.10, ...), custom_call_target="tpu_custom_call" | custom-call | tf_op jit(solution)/shard_map/form/pallas_call | solution.py:420
  75.3 0.1 collective-permute-start.11
  75.4 2.0 %collective-permute-done.11 = f32[16,72,128]{2,1,0:T(8,128)S(1)} collective-permute-done((f32[16,72,128]{2,1,0:T(8,128)S(1)}, f32[16,72,128]{2,1,0:T(8,128)S(1)}, u32[]{:S(2)}, u32[]{:S(2)}) %collective-permute-start.11) | collective-permute-done | bytes 589856 | tf_op jit(solution)/shard_map/ppermute | solution.py:465
  77.4 0.1 add.31
  77.5 15.4 %all_to_all.10.arrived = f32[16,72,128]{2,1,0:T(8,128)S(1)} all-to-all(f32[16,72,128]{2,1,0:T(8,128)S(1)} %add.31), channel_id=1, replica_groups={{0,8,16,24,32,40,48,56,64,72,80,88,96,104,112,120},{4,12,20,28,36,44,52..., dimensions={0} | all-to-all | bytes 1179648 | tf_op jit(solution)/shard_map/all_to_all | solution.py:465
  92.9 0.1 update.1
  93.0 14.8 %all_to_all.11.mine = f32[16,72,128]{2,1,0:T(8,128)S(1)} all-to-all(f32[16,72,128]{2,1,0:T(8,128)S(1)} %update.1), channel_id=1, replica_groups={{0,8,16,24,32,40,48,56,64,72,80,88,96,104,112,120},{4,12,20,28,36,44,52..., dimensions={0} | all-to-all | bytes 1179648 | tf_op jit(solution)/shard_map/all_to_all | solution.py:474
  107.8 2.0 %collective-permute-done.12.other = f32[16,72,128]{2,1,0:T(8,128)S(1)} collective-permute-done((f32[16,72,128]{2,1,0:T(8,128)S(1)}, f32[16,72,128]{2,1,0:T(8,128)S(1)}, u32[]{:S(2)}, u32[]{:S(2)}) %collective-permute-start.12) | collective-permute-done | bytes 589856 | tf_op jit(solution)/shard_map/ppermute | solution.py:475
  109.8 3.7 %refine.1 = (f32[16,64,2048]{2,1,0:T(8,128)S(1)}, f32[16,128]{1,0:T(8,128)S(1)}, f32[16,128]{1,0:T(8,128)}) custom-call(f32[16,72,128]{2,1,0:T(8,128)S(1)} %all_to_all.11.mine, f32[16,72,128]{2,1,0:T(8,128)S(1)} %collective-permute-done.12.other, bf16[16,256,2048]{2,1,0:T(8,128)(2,1)S(1)} %get-tuple-element.14.formed), custom_call_target="tpu_custom_call" | custom-call | tf_op jit(solution)/shard_map/refine/pallas_call | solution.py:477
  113.5 0.1 collective-permute-start.13
  113.7 1.0 collective-permute-done.13
  114.7 1.2 collective-permute-start.16
  115.9 1.5 %collective-permute-start.15 = (f32[16,128]{1,0:T(8,128)S(1)}, f32[16,128]{1,0:T(8,128)S(1)}, u32[]{:S(2)}, u32[]{:S(2)}) collective-permute-start(f32[16,128]{1,0:T(8,128)S(1)} %add.32), channel_id=1, source_target_pairs={{0,16},{4,20},{8,24},{12,28},{16,0},{20,4},{24,8},{28,12},{32,48},... | collective-permute-start | bytes 24584 | tf_op jit(solution)/shard_map/ppermute | solution.py:511
  117.4 0.1 collective-permute-start.14
  117.5 0.9 collective-permute-done.16
  118.4 2.7 %collective-permute-done.15 = f32[16,128]{1,0:T(8,128)S(1)} collective-permute-done((f32[16,128]{1,0:T(8,128)S(1)}, f32[16,128]{1,0:T(8,128)S(1)}, u32[]{:S(2)}, u32[]{:S(2)}) %collective-permute-start.15) | collective-permute-done | bytes 8224 | tf_op jit(solution)/shard_map/ppermute | solution.py:511
  121.0 1.2 collective-permute-done.14
  122.3 1.1 collective-permute-start.19
  123.4 1.5 %collective-permute-start.18 = (f32[16,128]{1,0:T(8,128)S(1)}, f32[16,128]{1,0:T(8,128)S(1)}, u32[]{:S(2)}, u32[]{:S(2)}) collective-permute-start(f32[16,128]{1,0:T(8,128)S(1)} %add_add_fusion.1.sums_a), channel_id=1, source_target_pairs={{0,64},{4,68},{8,72},{12,76},{16,80},{20,84},{24,88},{28,92},{32,9... | collective-permute-start | bytes 24584 | tf_op jit(solution)/shard_map/ppermute | solution.py:513
  124.9 1.1 collective-permute-done.19.sums_d
  125.9 2.6 %collective-permute-done.18.sums_c = f32[16,128]{1,0:T(8,128)S(1)} collective-permute-done((f32[16,128]{1,0:T(8,128)S(1)}, f32[16,128]{1,0:T(8,128)S(1)}, u32[]{:S(2)}, u32[]{:S(2)}) %collective-permute-start.18) | collective-permute-done | bytes 8224 | tf_op jit(solution)/shard_map/ppermute | solution.py:513
  128.5 1.2 collective-permute-done.17.sums_b
  129.7 3.5 %scale.1 = f32[16,64,2048]{2,1,0:T(8,128)} custom-call(f32[16,128]{1,0:T(8,128)S(1)} %add_add_fusion.1.sums_a, f32[16,128]{1,0:T(8,128)S(1)} %collective-permute-done.17.sums_b, f32[16,128]{1,0:T(8,128)S(1)} %collective-permute-done.18.sums_c, f32[16,128]{1,0:T(8,128)S(1)} %collective-permute-done.19.sums_d, f32[16,64,2048]{2,1,0:T(8,128)S(1)} %get-tuple-element.16.updated), custom_call_target="tpu_custom_call" | custom-call | tf_op jit(solution)/shard_map/scale/pallas_call | solution.py:489
  (38 shorter events, 0.1 us)
Async XLA Ops:
  0.6 7.7 %copy-start.2 = (s32[2048]{0:T(1024)S(1)}, s32[2048]{0:T(1024)}, u32[]{:S(2)}) copy-start(s32[2048]{0:T(1024)} %param.11) | copy-start | bytes 24580
  0.6 7.7 %copy-start.1 = (f32[2048]{0:T(1024)S(1)}, f32[2048]{0:T(1024)}, u32[]{:S(2)}) copy-start(f32[2048]{0:T(1024)} %param.10) | copy-start | bytes 24580
  0.7 7.7 %copy-start.6 = (s32[16,256]{1,0:T(8,128)S(1)}, s32[16,256]{1,0:T(8,128)}, u32[]{:S(2)}) copy-start(s32[16,256]{1,0:T(8,128)} %order_hbm.1) | copy-start | bytes 49156
  0.7 7.7 %copy-start.5 = (f32[16,256]{1,0:T(8,128)S(1)}, f32[16,256]{1,0:T(8,128)}, u32[]{:S(2)}) copy-start(f32[16,256]{1,0:T(8,128)} %roots_hbm.1) | copy-start | bytes 49156
  0.7 7.7 %copy-start = (f32[2048]{0:T(1024)S(1)}, f32[2048]{0:T(1024)}, u32[]{:S(2)}) copy-start(f32[2048]{0:T(1024)} %param.9) | copy-start | bytes 24580
  2.5 35.7 %collective-permute-start.10 = (bf16[1024,512]{1,0:T(8,128)(2,1)S(1)}, bf16[1024,512]{1,0:T(8,128)(2,1)S(1)}, u32[]{:S(2)}, u32[]{:S(2)}) collective-permute-start(bf16[1024,512]{1,0:T(8,128)(2,1)S(1)} %pad_maximum_fusion), channel_id=1, source_target_pairs={{0,124},{4,0},{8,4},{12,8},{16,12},{20,16},{24,20},{28,24},{32,28}... | collective-permute-start | bytes 3145736 | tf_op jit(solution)/shard_map/ppermute | solution.py:390
  17.3 0.6 copy-start.3
  17.9 1.2 collective-permute-start
  17.9 20.3 %collective-permute-start.9 = (bf16[512,512]{1,0:T(8,128)(2,1)S(1)}, bf16[512,512]{1,0:T(8,128)(2,1)S(1)}, u32[]{:S(2)}, u32[]{:S(2)}) collective-permute-start(bf16[512,512]{1,0:T(8,128)(2,1)S(1)} %get-tuple-element.19), channel_id=1, source_target_pairs={{0,4},{4,8},{8,12},{12,16},{16,20},{20,24},{24,28},{28,32},{32,36}... | collective-permute-start | bytes 1572872 | tf_op jit(solution)/shard_map/ppermute | solution.py:389
  19.1 3.7 %collective-permute-start.3 = (f32[32,128]{1,0:T(8,128)S(1)}, f32[32,128]{1,0:T(8,128)S(1)}, u32[]{:S(2)}, u32[]{:S(2)}) collective-permute-start(f32[32,128]{1,0:T(8,128)S(1)} %add.27), channel_id=1, source_target_pairs={{0,24},{4,28},{8,0},{12,4},{16,8},{20,12},{24,16},{28,20},{32,56},... | collective-permute-start | bytes 49160 | tf_op jit(solution)/shard_map/ppermute | solution.py:511
  19.1 7.8 %collective-permute-start.2 = (f32[32,128]{1,0:T(8,128)S(1)}, f32[32,128]{1,0:T(8,128)S(1)}, u32[]{:S(2)}, u32[]{:S(2)}) collective-permute-start(f32[32,128]{1,0:T(8,128)S(1)} %add.27), channel_id=1, source_target_pairs={{0,16},{4,20},{8,24},{12,28},{16,0},{20,4},{24,8},{28,12},{32,48},... | collective-permute-start | bytes 49160 | tf_op jit(solution)/shard_map/ppermute | solution.py:511
  19.2 7.7 %collective-permute-start.1 = (f32[32,128]{1,0:T(8,128)S(1)}, f32[32,128]{1,0:T(8,128)S(1)}, u32[]{:S(2)}, u32[]{:S(2)}) collective-permute-start(f32[32,128]{1,0:T(8,128)S(1)} %add.27), channel_id=1, source_target_pairs={{0,8},{4,12},{8,16},{12,20},{16,24},{20,28},{24,0},{28,4},{32,40},... | collective-permute-start | bytes 49160 | tf_op jit(solution)/shard_map/ppermute | solution.py:511
  22.8 5.5 %collective-permute-start.8 = (f32[2,512]{1,0:T(2,128)S(1)}, f32[2,512]{1,0:T(2,128)S(1)}, u32[]{:S(2)}, u32[]{:S(2)}) collective-permute-start(f32[2,512]{1,0:T(2,128)S(1)} %get-tuple-element.20), channel_id=1, source_target_pairs={{0,124},{4,0},{8,4},{12,8},{16,12},{20,16},{24,20},{28,24},{32,28}... | collective-permute-start | bytes 12296 | tf_op jit(solution)/shard_map/ppermute | solution.py:394
  26.9 6.4 %collective-permute-start.7 = (f32[2,512]{1,0:T(2,128)S(1)}, f32[2,512]{1,0:T(2,128)S(1)}, u32[]{:S(2)}, u32[]{:S(2)}) collective-permute-start(f32[2,512]{1,0:T(2,128)S(1)} %get-tuple-element.21), channel_id=1, source_target_pairs={{0,4},{4,8},{8,12},{12,16},{16,20},{20,24},{24,28},{28,32},{32,36}... | collective-permute-start | bytes 12296 | tf_op jit(solution)/shard_map/ppermute | solution.py:393
  26.9 11.3 %copy-start.9 = (f32[32,128]{1,0:T(8,128)}, f32[32,128]{1,0:T(8,128)S(1)}, u32[]{:S(2)}) copy-start(f32[32,128]{1,0:T(8,128)S(1)} %add_add_fusion.squares_a) | copy-start | bytes 49156
  26.9 6.3 %collective-permute-start.6 = (f32[32,128]{1,0:T(8,128)S(1)}, f32[32,128]{1,0:T(8,128)S(1)}, u32[]{:S(2)}, u32[]{:S(2)}) collective-permute-start(f32[32,128]{1,0:T(8,128)S(1)} %add_add_fusion.squares_a), channel_id=1, source_target_pairs={{0,96},{4,100},{8,104},{12,108},{16,112},{20,116},{24,120},{28,124... | collective-permute-start | bytes 49160 | tf_op jit(solution)/shard_map/ppermute | solution.py:513
  28.3 9.9 %copy-start.13 = (f32[2,512]{1,0:T(2,128)}, f32[2,512]{1,0:T(2,128)S(1)}, u32[]{:S(2)}) copy-start(f32[2,512]{1,0:T(2,128)S(1)} %collective-permute-done.8.pair_after) | copy-start | bytes 12292
  28.3 5.2 %collective-permute-start.5 = (f32[32,128]{1,0:T(8,128)S(1)}, f32[32,128]{1,0:T(8,128)S(1)}, u32[]{:S(2)}, u32[]{:S(2)}) collective-permute-start(f32[32,128]{1,0:T(8,128)S(1)} %add_add_fusion.squares_a), channel_id=1, source_target_pairs={{0,64},{4,68},{8,72},{12,76},{16,80},{20,84},{24,88},{28,92},{32,9... | collective-permute-start | bytes 49160 | tf_op jit(solution)/shard_map/ppermute | solution.py:513
  33.2 5.0 %copy-start.14 = (f32[2,512]{1,0:T(2,128)}, f32[2,512]{1,0:T(2,128)S(1)}, u32[]{:S(2)}) copy-start(f32[2,512]{1,0:T(2,128)S(1)} %collective-permute-done.7.pair_before) | copy-start | bytes 12292
  33.2 4.9 %collective-permute-start.4 = (f32[32,128]{1,0:T(8,128)S(1)}, f32[32,128]{1,0:T(8,128)S(1)}, u32[]{:S(2)}, u32[]{:S(2)}) collective-permute-start(f32[32,128]{1,0:T(8,128)S(1)} %add_add_fusion.squares_a), channel_id=1, source_target_pairs={{0,32},{4,36},{8,40},{12,44},{16,48},{20,52},{24,56},{28,60},{32,6... | collective-permute-start | bytes 49160 | tf_op jit(solution)/shard_map/ppermute | solution.py:513
  33.2 5.0 %copy-start.10 = (f32[32,128]{1,0:T(8,128)}, f32[32,128]{1,0:T(8,128)S(1)}, u32[]{:S(2)}) copy-start(f32[32,128]{1,0:T(8,128)S(1)} %collective-permute-done.6.squares_d) | copy-start | bytes 49156
  33.6 4.7 %copy-start.11 = (f32[32,128]{1,0:T(8,128)}, f32[32,128]{1,0:T(8,128)S(1)}, u32[]{:S(2)}) copy-start(f32[32,128]{1,0:T(8,128)S(1)} %collective-permute-done.5.squares_c) | copy-start | bytes 49156
  38.2 0.6 copy-start.12
  38.2 0.8 copy-start.8
  38.2 1.1 copy-start.7
  39.3 53.6 %copy-start.4 = (f32[32,128]{1,0:T(8,128)S(1)}, f32[32,128]{1,0:T(8,128)}, u32[]{:S(2)}) copy-start(f32[32,128]{1,0:T(8,128)} %copy-done.3) | copy-start | bytes 49156
  75.3 2.1 %collective-permute-start.11 = (f32[16,72,128]{2,1,0:T(8,128)S(1)}, f32[16,72,128]{2,1,0:T(8,128)S(1)}, u32[]{:S(2)}, u32[]{:S(2)}) collective-permute-start(f32[16,72,128]{2,1,0:T(8,128)S(1)} %get-tuple-element.13), channel_id=1, source_target_pairs={{0,4},{4,0},{8,12},{12,8},{16,20},{20,16},{24,28},{28,24},{32,36},... | collective-permute-start | bytes 1769480 | tf_op jit(solution)/shard_map/ppermute | solution.py:465
  107.8 2.0 %collective-permute-start.12 = (f32[16,72,128]{2,1,0:T(8,128)S(1)}, f32[16,72,128]{2,1,0:T(8,128)S(1)}, u32[]{:S(2)}, u32[]{:S(2)}) collective-permute-start(f32[16,72,128]{2,1,0:T(8,128)S(1)} %all_to_all.11.mine), channel_id=1, source_target_pairs={{0,4},{4,0},{8,12},{12,8},{16,20},{20,16},{24,28},{28,24},{32,36},... | collective-permute-start | bytes 1769480 | tf_op jit(solution)/shard_map/ppermute | solution.py:475
  113.5 1.2 collective-permute-start.13
  114.7 3.7 %collective-permute-start.16 = (f32[16,128]{1,0:T(8,128)S(1)}, f32[16,128]{1,0:T(8,128)S(1)}, u32[]{:S(2)}, u32[]{:S(2)}) collective-permute-start(f32[16,128]{1,0:T(8,128)S(1)} %add.32), channel_id=1, source_target_pairs={{0,24},{4,28},{8,0},{12,4},{16,8},{20,12},{24,16},{28,20},{32,56},... | collective-permute-start | bytes 24584 | tf_op jit(solution)/shard_map/ppermute | solution.py:511
  115.9 5.2 %collective-permute-start.15 = (f32[16,128]{1,0:T(8,128)S(1)}, f32[16,128]{1,0:T(8,128)S(1)}, u32[]{:S(2)}, u32[]{:S(2)}) collective-permute-start(f32[16,128]{1,0:T(8,128)S(1)} %add.32), channel_id=1, source_target_pairs={{0,16},{4,20},{8,24},{12,28},{16,0},{20,4},{24,8},{28,12},{32,48},... | collective-permute-start | bytes 24584 | tf_op jit(solution)/shard_map/ppermute | solution.py:511
  117.4 4.9 %collective-permute-start.14 = (f32[16,128]{1,0:T(8,128)S(1)}, f32[16,128]{1,0:T(8,128)S(1)}, u32[]{:S(2)}, u32[]{:S(2)}) collective-permute-start(f32[16,128]{1,0:T(8,128)S(1)} %add.32), channel_id=1, source_target_pairs={{0,8},{4,12},{8,16},{12,20},{16,24},{20,28},{24,0},{28,4},{32,40},... | collective-permute-start | bytes 24584 | tf_op jit(solution)/shard_map/ppermute | solution.py:511
  122.3 3.7 %collective-permute-start.19 = (f32[16,128]{1,0:T(8,128)S(1)}, f32[16,128]{1,0:T(8,128)S(1)}, u32[]{:S(2)}, u32[]{:S(2)}) collective-permute-start(f32[16,128]{1,0:T(8,128)S(1)} %add_add_fusion.1.sums_a), channel_id=1, source_target_pairs={{0,96},{4,100},{8,104},{12,108},{16,112},{20,116},{24,120},{28,124... | collective-permute-start | bytes 24584 | tf_op jit(solution)/shard_map/ppermute | solution.py:513
  123.4 5.2 %collective-permute-start.18 = (f32[16,128]{1,0:T(8,128)S(1)}, f32[16,128]{1,0:T(8,128)S(1)}, u32[]{:S(2)}, u32[]{:S(2)}) collective-permute-start(f32[16,128]{1,0:T(8,128)S(1)} %add_add_fusion.1.sums_a), channel_id=1, source_target_pairs={{0,64},{4,68},{8,72},{12,76},{16,80},{20,84},{24,88},{28,92},{32,9... | collective-permute-start | bytes 24584 | tf_op jit(solution)/shard_map/ppermute | solution.py:513
  124.9 4.9 %collective-permute-start.17 = (f32[16,128]{1,0:T(8,128)S(1)}, f32[16,128]{1,0:T(8,128)S(1)}, u32[]{:S(2)}, u32[]{:S(2)}) collective-permute-start(f32[16,128]{1,0:T(8,128)S(1)} %add_add_fusion.1.sums_a), channel_id=1, source_target_pairs={{0,32},{4,36},{8,40},{12,44},{16,48},{20,52},{24,56},{28,60},{32,6... | collective-permute-start | bytes 24584 | tf_op jit(solution)/shard_map/ppermute | solution.py:513
